TPU v7x, 128 devices: a whole 4x4x4 slice. The times are simulated.
128 devices in a mesh: seq: 8 (over y, z_lo), chan: 16 (over z_hi, x, core).
Axes of the slice: x: 4, y: 4, z: 4 (z_hi: 2, z_lo: 2; z = z_hi * 2 + z_lo), core: 2. Of those that a mesh axis runs over, the one named last changes fastest.
Arguments:
- conv_input: bfloat16 [8192, 4096], P('seq', 'chan'), may hold values from -0.0078125 to 0.0078125
- grad_out: bfloat16 [8192, 4096], P(('seq', 'chan')), may hold values from -6 to 6
- out_weight: bfloat16 [4096, 4096], P('chan'), may hold values from -0.09375 to 0.09375
- filters: bfloat16 [128, 8192], P('chan'), may hold values from -0.0625 to 0.0625
Outputs:
- grad_input: bfloat16 [8192, 4096], P('seq', 'chan')
- grad_filters: float32 [128, 8192], P('chan', 'seq')
All inputs are finite; a program needn't handle non-finite values.
Results may differ from a plain program's by a relative error of at most 0.0051.
Values may be sent and summed in bfloat16 or wider, within the bound.
No kernel may reach another device: no remote copies, remote signals or barrier semaphores. Data moves between devices by JAX's collectives and lax.ppermute only.
A program may use at most 512 MiB of HBM per device.

v0:
```python
import jax
import jax.numpy as jnp
from jax import lax
from jax.sharding import PartitionSpec as P

BLK = 128


def shifted(array, axis, by):
    devices = lax.axis_size(axis)
    pairs = [(i, i + by) for i in range(devices) if 0 <= i + by < devices]
    return lax.ppermute(array, axis, pairs)


def toeplitz_tile(vector, tile_rows):
    group_count = vector.shape[0]
    spread = jnp.broadcast_to(vector[:, None, :], (group_count, tile_rows, 2 * tile_rows))
    flat_rows = spread.reshape(group_count, 2 * tile_rows * tile_rows)[
        :, : tile_rows * (2 * tile_rows - 1)
    ]
    return flat_rows.reshape(group_count, tile_rows, 2 * tile_rows - 1)[:, :, tile_rows - 1 :]


def diagonal_sums(products):
    group_count = products.shape[0]
    tile_rows = products.shape[1]
    flipped = jnp.pad(products[:, ::-1, :], ((0, 0), (0, 0), (0, tile_rows)))
    flat_rows = flipped.reshape(group_count, 2 * tile_rows * tile_rows)[
        :, : tile_rows * (2 * tile_rows - 1)
    ]
    return jnp.sum(flat_rows.reshape(group_count, tile_rows, 2 * tile_rows - 1), axis=1)


def tile_stack(filter_rows, offset_count):
    group_count = filter_rows.shape[0]
    padded_filter = jnp.pad(filter_rows, ((0, 0), (BLK, 5 * BLK)))
    blocks = padded_filter[:, 1 : 1 + (offset_count + 1) * BLK].reshape(
        group_count, offset_count + 1, BLK
    )
    vectors = jnp.concatenate([blocks[:, :-1], blocks[:, 1:]], axis=2)
    tiles = toeplitz_tile(vectors.reshape(group_count * offset_count, 2 * BLK), BLK)
    return tiles.reshape(group_count, offset_count, BLK, BLK).transpose(1, 0, 2, 3)


def channel_grads(input_major, later_major, filter_rows):
    group_count = filter_rows.shape[0]
    lag_count = filter_rows.shape[1]
    group_width = input_major.shape[0] // group_count
    row_count = input_major.shape[1]
    block_count = row_count // BLK
    offset_count = lag_count // BLK + 4
    tiles = tile_stack(filter_rows, offset_count)
    input_tiles = input_major.reshape(group_count, group_width, block_count, BLK)

    def one_offset(grad_acc, items):
        offset, matrix = items
        window = lax.dynamic_slice_in_dim(later_major, offset * BLK, row_count, 1)
        window = window.reshape(group_count, group_width, block_count, BLK)
        grad_acc = grad_acc + jnp.einsum(
            "gsr,gcar->gcas", matrix, window, preferred_element_type=jnp.float32
        )
        products = jnp.einsum(
            "gcas,gcar->gsr", input_tiles, window, preferred_element_type=jnp.float32
        )
        return (grad_acc, products)

    start_acc = jnp.zeros((group_count, group_width, block_count, BLK), jnp.float32)
    offsets = jnp.arange(offset_count, dtype=jnp.int32)
    grad_acc, products = lax.scan(one_offset, start_acc, (offsets, tiles), unroll=4)
    stacked = products.transpose(1, 0, 2, 3).reshape(group_count * offset_count, BLK, BLK)
    sums = jnp.pad(diagonal_sums(stacked), ((0, 0), (0, 1)))
    sums = sums.reshape(group_count, offset_count, 2, BLK)
    total = jnp.pad(sums[:, :, 0], ((0, 0), (0, 1), (0, 0))) + jnp.pad(
        sums[:, :, 1], ((0, 0), (1, 0), (0, 0))
    )
    flat_total = total.reshape(group_count, (offset_count + 1) * BLK)
    return (
        grad_acc.reshape(group_count * group_width, row_count),
        flat_total[:, BLK - 1 : BLK - 1 + lag_count],
    )


def on_device(conv_input, grad_out, out_weight, filters):
    grad_major = lax.dot_general(
        out_weight,
        lax.all_gather(grad_out, "chan", axis=0, tiled=True),
        (((1,), (1,)), ((), ())),
        preferred_element_type=jnp.float32,
    ).astype(jnp.bfloat16)
    row_count = conv_input.shape[0]
    lag_count = filters.shape[1]
    input_major = conv_input.T
    reach_count = min(lag_count // row_count, lax.axis_size("seq") - 1)
    pieces = [grad_major]
    moving = grad_major
    for step_index in range(reach_count):
        moving = shifted(moving, "seq", -1)
        pieces.append(moving)
    filler_rows = row_count + lag_count + 4 * BLK - row_count * (reach_count + 1)
    pieces.append(jnp.zeros((grad_major.shape[0], filler_rows), jnp.bfloat16))
    later_major = jnp.concatenate(pieces, axis=1)
    grad_local, filter_part = channel_grads(input_major, later_major, filters)
    grad_input = grad_local.astype(jnp.bfloat16).T
    grad_filters = lax.psum_scatter(filter_part, "seq", scatter_dimension=1, tiled=True)
    return (grad_input, grad_filters)


def solution(mesh):
    in_specs = (P("seq", "chan"), P(("seq", "chan"), None), P("chan", None), P("chan", None))
    out_specs = (P("seq", "chan"), P("chan", "seq"))
    return jax.shard_map(
        on_device, mesh=mesh, in_specs=in_specs, out_specs=out_specs, check_vma=False
    )
```

profile of v0, /device:TPU:0, one launch (start us, length us, event | category | flops | bytes accessed | tf_op | source)
XLA Modules:
  0.0 1315.0 jit_solution(17316141651400574267)
XLA Ops:
  8.0 77.8 %all-gather.2.cloned.1.call-done = bf16[1024,4096]{1,0:T(8,128)(2,1)} async-done(((bf16[64,4096]{1,0:T(8,128)(2,1)}), bf16[1024,4096]{1,0:T(8,128)(2,1)}) %all-gather.2.cloned.1.call-update) | async-done | bytes 8388624 | tf_op jit(solution)/shard_map/all_gather | solution.py:86
  85.8 6.6 constant_dynamic-update-slice_fusion.8
  93.6 14.7 %collective-permute-done = bf16[256,1024]{1,0:T(8,128)(2,1)S(1)} collective-permute-done((bf16[256,1024]{1,0:T(8,128)(2,1)S(1)}, bf16[256,1024]{1,0:T(8,128)(2,1)S(1)}, u32[]{:S(2)}, u32[]{:S(2)}) %collective-permute-start) | collective-permute-done | bytes 524320 | tf_op jit(solution)/shard_map/ppermute | solution.py:12
  109.6 13.8 %collective-permute-done.1 = bf16[256,1024]{1,0:T(8,128)(2,1)S(1)} collective-permute-done((bf16[256,1024]{1,0:T(8,128)(2,1)S(1)}, bf16[256,1024]{1,0:T(8,128)(2,1)S(1)}, u32[]{:S(2)}, u32[]{:S(2)}) %collective-permute-start.1) | collective-permute-done | bytes 524320 | tf_op jit(solution)/shard_map/ppermute | solution.py:12
  124.7 13.7 %collective-permute-done.2 = bf16[256,1024]{1,0:T(8,128)(2,1)S(1)} collective-permute-done((bf16[256,1024]{1,0:T(8,128)(2,1)S(1)}, bf16[256,1024]{1,0:T(8,128)(2,1)S(1)}, u32[]{:S(2)}, u32[]{:S(2)}) %collective-permute-start.2) | collective-permute-done | bytes 524320 | tf_op jit(solution)/shard_map/ppermute | solution.py:12
  139.6 13.0 collective-permute-done.3
  154.0 12.1 collective-permute-done.4
  168.8 11.5 broadcast_in_dim.36
  180.3 32.8 %copy.65 = bf16[68,8,128,256]{3,1,2,0:T(8,128)(2,1)} copy(bf16[68,8,128,256]{3,2,1,0:T(8,128)(2,1)} %bitcast.210) | data formatting | bytes 71303168
  213.0 24.1 %slice.78 = bf16[544,32640]{1,0:T(8,128)(2,1)} slice(bf16[544,32768]{1,0:T(8,128)(2,1)} %bitcast.211), slice={[0:544], [0:32640]} | slice | bytes 71024640 | tf_op jit(solution)/shard_map/slice | solution.py:18
  237.1 118.1 %reshape.91 = bf16[544,128,255]{2,1,0:T(8,128)(2,1)} reshape(bf16[544,32640]{1,0:T(8,128)(2,1)} %slice.78) | data formatting | bytes 71024640 | tf_op jit(solution)/shard_map/reshape | solution.py:21
  355.2 21.8 %slice.79 = bf16[544,128,128]{2,1,0:T(8,128)(2,1)} slice(bf16[544,128,255]{2,1,0:T(8,128)(2,1)} %reshape.91), slice={[0:544], [0:128], [127:255]} | slice | bytes 35651584 | tf_op jit(solution)/shard_map/slice | solution.py:21
  385.5 5.7 collective-permute-done.6
  393.1 325.1 %while.13 = (s32[]{:T(128)}, f32[8,32,8,128]{3,2,1,0:T(8,128)}, f32[17,4,8,128,128]{4,3,1,0,2:T(8,128)}, s32[17,4]{0,1:T(4,128)S(1)}, bf16[256,9728]{1,0:T(8,128...) while((s32[]{:T(128)}, f32[8,32,8,128]{3,2,1,0:T(8,128)}, ...), condition=%wide.region_1.2_spmd.clone, body=%wide.region_0.1_spmd.clone.sunk | while | flops 539754496 | bytes 45089340 | solution.py:69
  446.1 2.4 convolution_add_fusion.11
  465.4 2.4 convolution_add_fusion.11
  599.3 2.4 convolution_add_fusion.11
  718.2 268.1 %rev.3 = f32[544,128,128]{2,1,0:T(8,128)} reverse(f32[544,128,128]{2,1,0:T(8,128)} %bitcast.220), dimensions={1} | reverse | bytes 71303168 | tf_op jit(solution)/shard_map/rev | solution.py:27
  986.3 34.5 %pad.21 = f32[544,128,256]{2,1,0:T(8,128)} pad(f32[544,128,128]{2,1,0:T(8,128)} %rev.3, f32[]{:T(128)} %constant.29.clone.1), padding=0_0x0_0x0_128 | pad | bytes 106954752 | tf_op jit(solution)/shard_map/jit(_pad)/pad | solution.py:27
  1020.9 59.7 %copy.68 = f32[68,8,128,256]{3,1,2,0:T(8,128)} copy(f32[68,8,128,256]{3,2,1,0:T(8,128)} %bitcast.93) | data formatting | bytes 142606336
  1080.5 46.7 %slice.80 = f32[544,32640]{1,0:T(8,128)} slice(f32[544,32768]{1,0:T(8,128)} %bitcast.94), slice={[0:544], [0:32640]} | slice | bytes 142049280 | tf_op jit(solution)/shard_map/slice | solution.py:28
  1127.2 113.5 %reshape.98 = f32[544,128,255]{2,1,0:T(8,128)} reshape(f32[544,32640]{1,0:T(8,128)} %slice.80) | data formatting | bytes 142049280 | tf_op jit(solution)/shard_map/reshape | solution.py:31
  1240.7 22.9 %reduce_sum.9 = f32[544,255]{1,0:T(8,128)} reduce(f32[544,128,255]{2,1,0:T(8,128)} %reshape.98, f32[]{:T(128)} %constant.29.clone.1), dimensions={1}, to_apply=%region_2.3 | reduce | flops 17617440 | bytes 71579520 | tf_op jit(solution)/shard_map/reduce_sum | solution.py:31
  1271.7 36.5 %reduce-scatter.2.cloned.1.call-done = f32[8,1024]{1,0:T(8,128)} async-done(((f32[8,8192]{1,0:T(8,128)}), f32[8,1024]{1,0:T(8,128)}) %reduce-scatter.2.cloned.1.call-update) | async-done | bytes 32784 | tf_op jit(solution)/shard_map/reduce_scatter | solution.py:104
  (459 shorter events, 299.9 us)
Async XLA Ops:
  7.2 78.6 %copy-start = (bf16[256,4096]{1,0:T(8,128)(2,1)S(1)}, bf16[256,4096]{1,0:T(8,128)(2,1)}, u32[]{:S(2)}) copy-start(bf16[256,4096]{1,0:T(8,128)(2,1)} %param.8) | copy-start | bytes 6291460
  7.2 78.6 %all-gather.2.cloned.1.call-start = ((), (), s32[]{:S(2)}) async-start(), calls=%async_computation.1 | async-start | bytes 8912896 | tf_op jit(solution)/shard_map/all_gather | solution.py:86
  7.9 146.0 %copy-start.9 = (bf16[8,8192]{1,0:T(8,128)(2,1)S(1)}, bf16[8,8192]{1,0:T(8,128)(2,1)}, u32[]{:S(2)}) copy-start(bf16[8,8192]{1,0:T(8,128)(2,1)} %param.9) | copy-start | bytes 393220
  7.9 159.7 %copy-start.5 = (bf16[1024,256]{1,0:T(8,128)(2,1)S(1)}, bf16[1024,256]{1,0:T(8,128)(2,1)}, u32[]{:S(2)}) copy-start(bf16[1024,256]{1,0:T(8,128)(2,1)} %param.6) | copy-start | bytes 1572868
  7.9 1300.3 %reduce-scatter.2.cloned.1.call-start = ((), (), s32[]{:S(2)}) async-start(), calls=%async_computation.2 | async-start | bytes 294912 | tf_op jit(solution)/shard_map/reduce_scatter | solution.py:104
  92.3 16.0 %collective-permute-start = (bf16[256,1024]{1,0:T(8,128)(2,1)S(1)}, bf16[256,1024]{1,0:T(8,128)(2,1)S(1)}, u32[]{:S(2)}, u32[]{:S(2)}) collective-permute-start(bf16[256,1024]{1,0:T(8,128)(2,1)S(1)} %get-tuple-element.120), channel_id=1, source_target_pairs={{16,0},{32,16},{48,32},{64,48},{80,64},{96,80},{112,96},{17,1},{33... | collective-permute-start | bytes 1572872 | tf_op jit(solution)/shard_map/ppermute | solution.py:12
  108.3 15.1 %collective-permute-start.1 = (bf16[256,1024]{1,0:T(8,128)(2,1)S(1)}, bf16[256,1024]{1,0:T(8,128)(2,1)S(1)}, u32[]{:S(2)}, u32[]{:S(2)}) collective-permute-start(bf16[256,1024]{1,0:T(8,128)(2,1)S(1)} %collective-permute-done), channel_id=1, source_target_pairs={{16,0},{32,16},{48,32},{64,48},{80,64},{96,80},{112,96},{17,1},{33... | collective-permute-start | bytes 1572872 | tf_op jit(solution)/shard_map/ppermute | solution.py:12
  123.4 14.9 %collective-permute-start.2 = (bf16[256,1024]{1,0:T(8,128)(2,1)S(1)}, bf16[256,1024]{1,0:T(8,128)(2,1)S(1)}, u32[]{:S(2)}, u32[]{:S(2)}) collective-permute-start(bf16[256,1024]{1,0:T(8,128)(2,1)S(1)} %collective-permute-done.1), channel_id=1, source_target_pairs={{16,0},{32,16},{48,32},{64,48},{80,64},{96,80},{112,96},{17,1},{33... | collective-permute-start | bytes 1572872 | tf_op jit(solution)/shard_map/ppermute | solution.py:12
  138.3 14.3 %collective-permute-start.3 = (bf16[256,1024]{1,0:T(8,128)(2,1)S(1)}, bf16[256,1024]{1,0:T(8,128)(2,1)S(1)}, u32[]{:S(2)}, u32[]{:S(2)}) collective-permute-start(bf16[256,1024]{1,0:T(8,128)(2,1)S(1)} %collective-permute-done.2), channel_id=1, source_target_pairs={{16,0},{32,16},{48,32},{64,48},{80,64},{96,80},{112,96},{17,1},{33... | collective-permute-start | bytes 1572872 | tf_op jit(solution)/shard_map/ppermute | solution.py:12
  152.6 13.5 %copy-start.7 = (bf16[256,1024]{1,0:T(8,128)(2,1)}, bf16[256,1024]{1,0:T(8,128)(2,1)S(1)}, u32[]{:S(2)}) copy-start(bf16[256,1024]{1,0:T(8,128)(2,1)S(1)} %collective-permute-done.3) | copy-start | bytes 1572868
  152.6 13.5 %collective-permute-start.4 = (bf16[256,1024]{1,0:T(8,128)(2,1)S(1)}, bf16[256,1024]{1,0:T(8,128)(2,1)}, u32[]{:S(2)}, u32[]{:S(2)}) collective-permute-start(bf16[256,1024]{1,0:T(8,128)(2,1)S(1)} %collective-permute-done.3), channel_id=1, source_target_pairs={{16,0},{32,16},{48,32},{64,48},{80,64},{96,80},{112,96},{17,1},{33... | collective-permute-start | bytes 1572872 | tf_op jit(solution)/shard_map/ppermute | solution.py:12
  166.1 211.7 %collective-permute-start.5 = (bf16[256,1024]{1,0:T(8,128)(2,1)}, bf16[256,1024]{1,0:T(8,128)(2,1)}, u32[]{:S(2)}, u32[]{:S(2)}) collective-permute-start(bf16[256,1024]{1,0:T(8,128)(2,1)} %collective-permute-done.4), channel_id=1, source_target_pairs={{16,0},{32,16},{48,32},{64,48},{80,64},{96,80},{112,96},{17,1},{33... | collective-permute-start | bytes 1572872 | tf_op jit(solution)/shard_map/ppermute | solution.py:12
  355.2 25.7 %copy-start.8 = (bf16[256,1024]{1,0:T(8,128)(2,1)S(1)}, bf16[256,1024]{1,0:T(8,128)(2,1)}, u32[]{:S(2)}) copy-start(bf16[256,1024]{1,0:T(8,128)(2,1)} %copy-done.7) | copy-start | bytes 1572868
  377.8 13.4 %collective-permute-start.6 = (bf16[256,1024]{1,0:T(8,128)(2,1)}, bf16[256,1024]{1,0:T(8,128)(2,1)S(1)}, u32[]{:S(2)}, u32[]{:S(2)}) collective-permute-start(bf16[256,1024]{1,0:T(8,128)(2,1)} %collective-permute-done.5), channel_id=1, source_target_pairs={{16,0},{32,16},{48,32},{64,48},{80,64},{96,80},{112,96},{17,1},{33... | collective-permute-start | bytes 1572872 | tf_op jit(solution)/shard_map/ppermute | solution.py:12
  415.0 2.6 copy-start.6
  453.3 2.6 copy-start.6
  472.6 2.6 copy-start.6
  530.0 2.6 copy-start.6
  606.5 2.7 copy-start.6
  664.0 2.5 copy-start.6
  683.2 2.5 copy-start.6
  702.3 2.5 copy-start.6
  1240.7 67.5 %copy-start.1 = (bf16[256,4096]{1,0:T(8,128)(2,1)S(1)}, bf16[256,4096]{1,0:T(8,128)(2,1)}, u32[]{:S(2)}) copy-start(bf16[256,4096]{1,0:T(8,128)(2,1)} %param.8) | copy-start | bytes 6291460
  1263.7 6.8 copy-start.4
  (43 other events, 62.1 us)
Sparse Core Ops, SparseCore 0:
  10.4 75.2 all-gather.1
  1270.6 37.5 reduce-scatter.1
where the time goes:
time: 1340 us; the launch traced here: 1320 us
  local copies, waits for them, and re-layouts  861 us (64%)
  waiting for transfers between devices  188 us (14%)
  matrix products  147 us (11%)
  other arithmetic  49 us (4%)
  loops' own time  46.4 us (3%)
  between operations  14.3 us (1%)
    rev x1, local copies, waits for them, and re-layouts, diagonal_sums(): flipped = jnp.pad(products[:, ::-1, :], ((0, 0), (0, 0), (0, tile_rows)))  268 us
    reshape x1, local copies, waits for them, and re-layouts, toeplitz_tile(): flat_rows.reshape(group_count, tile_rows, 2 * tile_rows - 1)  118 us
    dot_general x68, matrix products, one_offset(): jnp.einsum('gsr,gcar->gcas', matrix, window, preferred_element_type=jnp.f...  116 us
    reshape x1, local copies, waits for them, and re-layouts, diagonal_sums(): flat_rows.reshape(group_count, tile_rows, 2 * tile_rows - 1)  114 us
    unnamed x28, local copies, waits for them, and re-layouts  103 us
    all_gather x1, waiting for transfers between devices, on_device(): lax.all_gather(grad_out, 'chan', axis=0, tiled=True)  77.8 us
    ppermute x7, waiting for transfers between devices, shifted(): return lax.ppermute(array, axis, pairs)  72.9 us
    dynamic_update_slice x34, local copies, waits for them, and re-layouts, channel_grads(): lax.scan(one_offset, start_acc, (offsets, tiles), unroll=4)  59.6 us
  transfers between devices with their start and end apart: 9, of which 8 were waited for; matrix products, arithmetic and copies ran while one was open for 17% of the time, Pallas kernels for 0%

commit v1 on v0

v1 whole, which is shorter than its diff:
```python
import functools

import jax
import jax.numpy as jnp
from jax import lax
from jax.experimental import pallas as pl
from jax.experimental.pallas import tpu as pltpu
from jax.sharding import Mesh
from jax.sharding import PartitionSpec as P

F32 = jnp.float32
BF16 = jnp.bfloat16

TILE = 128
BLK = 256
PART = 16
TAIL = 8
VMEM_MIB = 24
X_UP = [(i, (i + 1) % 4) for i in range(4)]
X_DOWN = [(i, (i - 1) % 4) for i in range(4)]
Z_NEAR = [(i, 3 - i) for i in range(4)]
SWAP = [(0, 1), (1, 0)]


def mm(a, b, dims=(((1,), (0,)), ((), ()))):
    return lax.dot_general(a, b, dims, preferred_element_type=F32)


def iota(shape, axis):
    return lax.broadcasted_iota(jnp.int32, shape, axis)


def params():
    return pltpu.CompilerParams(vmem_limit_bytes=VMEM_MIB * 2**20)


def cost(flops, moved):
    return pl.CostEstimate(flops=flops, bytes_accessed=moved, transcendentals=0)


def prep_body(x_ref, o_ref, *, groups, width):
    blocks = x_ref.shape[0] // BLK
    chans = x_ref.shape[1]
    flip = (iota((BLK, BLK), 0) + iota((BLK, BLK), 1) == BLK - 1).astype(BF16)
    turned = [
        mm(flip, x_ref[a * BLK : (a + 1) * BLK, :]).astype(BF16) for a in range(blocks)
    ]
    row = iota((chans, TILE), 0)
    col = iota((chans, TILE), 1)
    for g in range(groups):
        total = jnp.zeros((BLK, TILE), F32)
        for a in range(blocks):
            pick = (row - g * width == col - a * width) & (col // width == a)
            total = total + mm(turned[a], pick.astype(BF16))
        o_ref[g] = total.astype(BF16)


def prep_input(x, groups, width):
    return pl.pallas_call(
        functools.partial(prep_body, groups=groups, width=width),
        out_shape=jax.ShapeDtypeStruct((groups, BLK, TILE), BF16),
        name="prep_input",
        compiler_params=params(),
        cost_estimate=cost(2 * 10**9, 4 * x.size),
    )(x)


def tiles_body(f_ref, x_ref, o_ref, y_ref):
    for s in range(x_ref.shape[0]):
        y_ref[:, s * TILE : (s + 1) * TILE] = x_ref[s]
    count = f_ref.shape[0]
    flip = (iota((TILE, TILE), 0) + iota((TILE, TILE), 1) == TILE - 1).astype(BF16)
    turned = mm(f_ref[...], flip)
    o_ref[0] = jnp.zeros((TILE, TILE), BF16)
    zero = jnp.zeros((1, TILE), F32)
    for k in range(count):
        before = turned[k - 1 : k] if k else zero
        line = jnp.concatenate([before, turned[k : k + 1]], axis=1)
        spread = jnp.broadcast_to(line, (TILE, 2 * TILE))
        turn = pltpu.roll(spread, 1, 1, stride=1, stride_axis=0)
        o_ref[k + 1] = turn[:, :TILE].astype(BF16)


def toeplitz_tiles(f, x):
    count = f.shape[0]
    return pl.pallas_call(
        tiles_body,
        out_shape=(
            jax.ShapeDtypeStruct((count + 1, TILE, TILE), BF16),
            jax.ShapeDtypeStruct((BLK, x.shape[0] * TILE), BF16),
        ),
        name="toeplitz_tiles",
        compiler_params=params(),
        cost_estimate=cost(2 * 10**9, 2 * count * TILE * TILE),
    )(f, x)


def project_body(s_ref, own_ref, other_ref, *refs, shifts):
    blocks, o_ref, rows, acc = refs[:-3], refs[-3], refs[-2], refs[-1]
    k = pl.program_id(0)
    x = s_ref[0]
    core = s_ref[1]
    chans = own_ref.shape[0]
    size = rows.shape[0] // 4
    for ref, (shift, at) in zip(blocks, shifts):
        spot = lax.rem(x + shift, 4) * size + at
        rows[pl.ds(pl.multiple_of(spot, 32), ref.shape[0]), :] = ref[...]

    @pl.when(k == 0)
    def _():
        acc[...] = jnp.zeros_like(acc)

    dims = (((1,), (1,)), ((), ()))
    acc[:chans, :] += mm(own_ref[...], rows[...], dims)
    acc[chans:, :] += mm(other_ref[...], rows[...], dims)

    @pl.when(k == pl.num_programs(0) - 1)
    def _():
        at = pl.multiple_of(core * chans, chans)
        o_ref[pl.ds(at, chans), :] = acc[:chans, :].astype(BF16)
        at = pl.multiple_of((1 - core) * chans, chans)
        o_ref[pl.ds(at, chans), :] = acc[chans:, :].astype(BF16)


def project(spots, own, other, blocks, shifts, steps=4):
    chans, depth = own.shape
    step = depth // steps
    rows = sum(b.shape[0] for b in blocks)
    return pl.pallas_call(
        functools.partial(project_body, shifts=shifts),
        out_shape=jax.ShapeDtypeStruct((2 * chans, rows), BF16),
        grid_spec=pltpu.PrefetchScalarGridSpec(
            num_scalar_prefetch=1,
            grid=(steps,),
            in_specs=[pl.BlockSpec((chans, step), lambda k, s: (0, k))] * 2
            + [pl.BlockSpec((b.shape[0], step), lambda k, s: (0, k)) for b in blocks],
            out_specs=pl.BlockSpec((2 * chans, rows), lambda k, s: (0, 0)),
            scratch_shapes=[
                pltpu.VMEM((rows, step), BF16),
                pltpu.VMEM((2 * chans, rows), F32),
            ],
        ),
        name="project",
        compiler_params=params(),
        cost_estimate=cost(4 * chans * rows * depth, 2 * depth * (2 * chans + rows)),
    )(spots, own, other, *blocks)


def conv_body(s_ref, g0_ref, g1_ref, x_ref, t_ref, o_ref, gb, acc, corr):
    zhi = s_ref[0]
    width = g0_ref.shape[1]
    senders = g0_ref.shape[0] // 2
    nb = 4 * senders
    top = nb * width
    lane = iota((width, TILE), 1)
    gb[top:, :] = jnp.zeros((gb.shape[0] - top, BLK), BF16)
    for half, g_ref in enumerate((g0_ref, g1_ref)):
        for s in range(senders):
            owner = s ^ half
            zz = 1 - zhi if half else zhi
            for xh in range(2):
                lo = xh * TILE
                a = g_ref[s, :, lo : lo + TILE].astype(F32)
                b = g_ref[senders + s, :, lo : lo + TILE].astype(F32)
                left = jnp.where(lane < 64, a, pltpu.roll(b, 64, 1))
                right = jnp.where(lane < 64, pltpu.roll(a, 64, 1), b)
                spot = (owner * 4 + zz * 2 + xh) * width
                at = pl.ds(pl.multiple_of(spot, width), width)
                gb[at, :TILE] = left.astype(BF16)
                gb[at, TILE:] = right.astype(BF16)

    def put(k, value, fresh=False):
        for part in range(TILE // PART):
            piece = value[part * PART : (part + 1) * PART, :]
            at = slice(k * PART, (k + 1) * PART)
            if fresh:
                corr[part, at, :] = piece
            else:
                corr[part, at, :] += piece

    for d in range(nb):
        span = -(-(nb - d) * width // BLK) * BLK
        moved = gb[d * width : d * width + span, :]
        mid = t_ref[2 * d + 1]
        up = t_ref[2 * d + 2]
        down = t_ref[2 * d]
        tile = jnp.concatenate(
            [
                jnp.concatenate([mid, down], axis=1),
                jnp.concatenate([up, mid], axis=1),
            ],
            axis=0,
        )
        if d == 0:
            acc[...] = mm(moved, tile)
        else:
            acc[:span, :] += mm(moved, tile)
        prod = mm(x_ref[:, :span], moved)
        put(2 * d, prod[:TILE, :TILE], fresh=d == 0)
        put(2 * d + 1, prod[:TILE, TILE:] + prod[TILE:, :TILE], fresh=True)
        put(2 * d + 2, prod[TILE:, TILE:], fresh=True)

    for s in range(senders):
        for k in range(4):
            a = s * 4 + k
            o_ref[s, :width, k * BLK : (k + 1) * BLK] = acc[
                a * width : (a + 1) * width, :
            ].astype(BF16)

    lane = iota((PART, TILE), 1)
    turned = lane <= iota((PART, TILE), 0)
    spill = jnp.zeros((PART, TILE), F32)
    carry = jnp.zeros((1, TILE), F32)
    lines = []
    for k in range(2 * nb + 2):
        total = spill
        if k <= 2 * nb:
            low = corr[0, k * PART : (k + 1) * PART, :]
            spill = jnp.zeros((PART, TILE), F32)
            for part in range(1, TILE // PART):
                by = part * PART
                move = pltpu.roll(corr[part, k * PART : (k + 1) * PART, :], by, 1)
                low = low + jnp.where(lane >= by, move, 0.0)
                spill = spill + jnp.where(lane < by, move, 0.0)
            total = total + low
        move = pltpu.roll(total, 1, 1, stride=1, stride_axis=0)
        line = jnp.sum(jnp.where(turned, 0.0, move), axis=0, keepdims=True)
        if k >= 2:
            lines.append(line + carry)
        carry = jnp.sum(jnp.where(turned, move, 0.0), axis=0, keepdims=True)

    for s in range(senders):
        rest = jnp.concatenate(lines[s * TAIL : (s + 1) * TAIL], axis=0)
        for part in range(3):
            piece = rest.astype(BF16)
            o_ref[s, width:, part * TILE : (part + 1) * TILE] = piece
            rest = rest - piece.astype(F32)
        o_ref[s, width:, 3 * TILE :] = jnp.zeros((TAIL, o_ref.shape[2] - 3 * TILE), BF16)


def convolve(spot, g0, g1, xt, tiles):
    senders = g0.shape[0] // 2
    width = g0.shape[1]
    nb = 4 * senders
    top = nb * width
    return pl.pallas_call(
        conv_body,
        out_shape=jax.ShapeDtypeStruct((senders, width + TAIL, 4 * BLK), BF16),
        in_specs=[pl.BlockSpec(memory_space=pltpu.SMEM)]
        + [pl.BlockSpec(memory_space=pltpu.VMEM)] * 4,
        scratch_shapes=[
            pltpu.VMEM((top + BLK, BLK), BF16),
            pltpu.VMEM((top, BLK), F32),
            pltpu.VMEM((TILE // PART, (2 * nb + 1) * PART, TILE), F32),
        ],
        name="convolve",
        compiler_params=params(),
        cost_estimate=cost(6 * 10**9, 4 * 10**6),
    )(spot, g0, g1, xt, tiles)


def finish_body(m_ref, o_ref, f_ref):
    groups, rows, _ = m_ref.shape
    width = rows - TAIL
    for g in range(groups // 4):
        four = [m_ref[4 * g + i, :width, :].astype(F32) for i in range(4)]
        flat = jnp.concatenate(four, axis=0)
        o_ref[:, g * TILE : (g + 1) * TILE] = flat.T.astype(BF16)
    for g in range(groups):
        rest = m_ref[g, width:, : 3 * TILE].astype(F32)
        total = rest[:, :TILE] + rest[:, TILE : 2 * TILE] + rest[:, 2 * TILE :]
        for j in range(TAIL):
            f_ref[g : g + 1, j * TILE : (j + 1) * TILE] = total[j : j + 1, :]


def finish(major):
    groups, rows, span = major.shape
    return pl.pallas_call(
        finish_body,
        out_shape=(
            jax.ShapeDtypeStruct((span, groups * (rows - TAIL)), BF16),
            jax.ShapeDtypeStruct((groups, TAIL * TILE), F32),
        ),
        name="finish",
        compiler_params=params(),
        cost_estimate=cost(10**6, 4 * major.size),
    )(major)


def on_device(conv_input, grad_out, out_weight, filters):
    groups = filters.shape[0]
    width = conv_input.shape[1] // groups
    seq = ("y", "zlo")
    near = ("zlo", "zhi")
    x = lax.axis_index("x").astype(jnp.int32)
    core = lax.axis_index("core").astype(jnp.int32)
    zhi = lax.axis_index("zhi").astype(jnp.int32)
    half = grad_out.shape[0] // 2
    before = lax.ppermute(grad_out, "x", X_UP)
    after = lax.ppermute(grad_out, "x", X_DOWN)
    other_weight = lax.ppermute(out_weight, "core", SWAP)
    near_own = lax.ppermute(grad_out, near, Z_NEAR)
    turned = prep_input(conv_input, groups, width)
    turned = lax.all_to_all(turned, seq, 0, 0, tiled=True)
    far_a = lax.ppermute(before[:half], "x", X_UP)
    far_b = lax.ppermute(after[half:], "x", X_DOWN)
    near_before = lax.ppermute(near_own, "x", X_UP)
    near_after = lax.ppermute(near_own, "x", X_DOWN)
    near_far_a = lax.ppermute(far_a, near, Z_NEAR)
    near_far_b = lax.ppermute(far_b, near, Z_NEAR)
    tap = lax.dynamic_index_in_dim(filters, lax.axis_index(seq), 0, False)
    tiles, xt = toeplitz_tiles(tap.reshape(-1, TILE), turned)
    spots = jnp.stack([x, core])
    shifts = [(0, 0), (3, 0), (1, 0), (2, 0), (2, half)]
    everyone = ("core",) + seq
    g0 = project(
        spots, out_weight, other_weight,
        [grad_out, before, after, far_a, far_b], shifts,
    )
    g0 = lax.all_to_all(g0.reshape(2 * groups, width, -1), everyone, 0, 0, tiled=True)
    g1 = project(
        spots, out_weight, other_weight,
        [near_own, near_before, near_after, near_far_a, near_far_b], shifts,
    )
    g1 = lax.all_to_all(g1.reshape(2 * groups, width, -1), everyone, 0, 0, tiled=True)
    major = convolve(zhi.reshape(1), g0, g1, xt, tiles)
    major = lax.all_to_all(major, seq, 0, 0, tiled=True)
    return finish(major)


def solution(mesh):
    fine = Mesh(
        mesh.devices.reshape(4, 2, 2, 4, 2),
        ("y", "zlo", "zhi", "x", "core"),
        axis_types=(jax.sharding.AxisType.Auto,) * 5,
    )
    seq = ("y", "zlo")
    chan = ("zhi", "x", "core")
    in_specs = (P(seq, chan), P(seq + chan, None), P(chan, None), P(chan, None))
    out_specs = (P(seq, chan), P(chan, seq))
    return jax.shard_map(
        on_device, mesh=fine, in_specs=in_specs, out_specs=out_specs, check_vma=False
    )
```

time: 1340 us -> 91.2 us (0.07); the launches traced: 1320 us -> 90.5 us
  local copies, waits for them, and re-layouts: 861 us -> 7.38 us
  waiting for transfers between devices: 188 us -> 14.9 us
  matrix products: 147 us -> 0 us
  other arithmetic: 49 us -> 0.07 us
  loops' own time: 46.4 us -> 0 us
  starting transfers between devices: 9.04 us -> 32.2 us
  Pallas kernels: 0 us -> 21.5 us
  blocking collectives: 0 us -> 13.6 us
  between operations: 14.3 us -> 0.77 us
    rev x1 -> x0, local copies, waits for them, and re-layouts: 268 us -> none  [diagonal_sums(): flipped = jnp.pad(products[:, ::-1, :], ((0, 0), (0, 0), (0, tile_rows)))]
    reshape x4 -> x0, local copies, waits for them, and re-layouts: 234 us -> none  [the longest x1 118 us: toeplitz_tile(): flat_rows.reshape(group_count, tile_rows, 2 * tile_rows - 1)]
    dot_general x137 -> x0, matrix products: 147 us -> none  [the longest x68 116 us: one_offset(): jnp.einsum('gsr,gcar->gcas', matrix, window, preferred_element_type=jnp.f...]
    slice x23 -> x2, local copies, waits for them, and re-layouts: 105 us -> 1.46 us  [the longest x1 0.73 us: on_device(): far_a = lax.ppermute(before[:half], 'x', X_UP)]
    unnamed x28 -> x14, local copies, waits for them, and re-layouts: 103 us -> 5.81 us
    all_gather x1 -> x0, waiting for transfers between devices: 77.8 us -> none  [on_device(): lax.all_gather(grad_out, 'chan', axis=0, tiled=True)]
    ppermute x7 -> x10, waiting for transfers between devices: 72.9 us -> 8.31 us  [the longest x1 8.29 us: on_device(): before = lax.ppermute(grad_out, 'x', X_UP)]
    dynamic_update_slice x34 -> x0, local copies, waits for them, and re-layouts: 59.6 us -> none  [channel_grads(): lax.scan(one_offset, start_acc, (offsets, tiles), unroll=4)]
  transfers between devices with their start and end apart: 9 -> 13, of which waited for: 8 -> 3; matrix products, arithmetic and copies ran while one was open for 17% -> 2% of each run, Pallas kernels for 0% -> 16%
where the time goes in v1:
time: 91.2 us; the launch traced here: 90.5 us
  starting transfers between devices  32.2 us (35%)
  Pallas kernels  21.5 us (24%)
  waiting for transfers between devices  14.9 us (16%)
  blocking collectives  13.6 us (15%)
  local copies, waits for them, and re-layouts  7.38 us (8%)
    all_to_all x1, blocking collectives, on_device(): major = lax.all_to_all(major, seq, 0, 0, tiled=True)  13.6 us
    pallas_call x2, Pallas kernels, project(): pl.pallas_call(functools.partial(project_body, shifts=shifts), out_shape=...  10.7 us
    ppermute x1, waiting for transfers between devices, on_device(): before = lax.ppermute(grad_out, 'x', X_UP)  8.29 us
    pallas_call x1, Pallas kernels, convolve(): pl.pallas_call(conv_body, out_shape=jax.ShapeDtypeStruct((senders, width...  5.98 us
    all_to_all x1, starting transfers between devices, on_device(): turned = lax.all_to_all(turned, seq, 0, 0, tiled=True)  5.94 us
    unnamed x14, local copies, waits for them, and re-layouts  5.81 us
    all_to_all x1, starting transfers between devices, on_device(): lax.all_to_all(g0.reshape(2 * groups, width, -1), everyone, 0, 0, tiled=T...  4.35 us
    ppermute x1, starting transfers between devices, on_device(): near_own = lax.ppermute(grad_out, near, Z_NEAR)  4.15 us
  transfers between devices with their start and end apart: 13, of which 3 were waited for; matrix products, arithmetic and copies ran while one was open for 2% of the time, Pallas kernels for 16%

profile of v1, /device:TPU:0, one launch (start us, length us, event | category | flops | bytes accessed | tf_op | source)
XLA Modules:
  0.0 90.5 jit_solution(9838286255413039205)
XLA Ops:
  0.7 1.7 %collective-permute-start.1 = (bf16[64,4096]{1,0:T(8,128)(2,1)}, bf16[64,4096]{1,0:T(8,128)(2,1)S(1)}, u32[]{:S(2)}, u32[]{:S(2)}) collective-permute-start(bf16[64,4096]{1,0:T(8,128)(2,1)} %refs_0_.1), channel_id=1, source_target_pairs={{0,2},{2,4},{4,6},{6,0},{1,3},{3,5},{5,7},{7,1},{8,10},{10,12},{12... | collective-permute-start | bytes 1572872 | tf_op jit(solution)/shard_map/ppermute | solution.py:299
  2.4 1.6 %collective-permute-start.2 = (bf16[64,4096]{1,0:T(8,128)(2,1)}, bf16[64,4096]{1,0:T(8,128)(2,1)S(1)}, u32[]{:S(2)}, u32[]{:S(2)}) collective-permute-start(bf16[64,4096]{1,0:T(8,128)(2,1)} %refs_0_.1), channel_id=1, source_target_pairs={{0,6},{2,0},{4,2},{6,4},{1,7},{3,1},{5,3},{7,5},{8,14},{10,8},{12,... | collective-permute-start | bytes 1572872 | tf_op jit(solution)/shard_map/ppermute | solution.py:300
  4.0 4.1 %collective-permute-start.5 = (bf16[64,4096]{1,0:T(8,128)(2,1)}, bf16[64,4096]{1,0:T(8,128)(2,1)}, u32[]{:S(2)}, u32[]{:S(2)}) collective-permute-start(bf16[64,4096]{1,0:T(8,128)(2,1)} %refs_0_.1), channel_id=1, source_target_pairs={{0,24},{8,16},{16,8},{24,0},{1,25},{9,17},{17,9},{25,1},{2,26},{10... | collective-permute-start | bytes 1572872 | tf_op jit(solution)/shard_map/ppermute | solution.py:302
  8.2 8.3 %collective-permute-done.1.refs_1_ = bf16[64,4096]{1,0:T(8,128)(2,1)S(1)} collective-permute-done((bf16[64,4096]{1,0:T(8,128)(2,1)}, bf16[64,4096]{1,0:T(8,128)(2,1)S(1)}, u32[]{:S(2)}, u32[]{:S(2)}) %collective-permute-start.1) | collective-permute-done | bytes 524320 | tf_op jit(solution)/shard_map/ppermute | solution.py:299
  18.3 2.8 %collective-permute-start.4 = (bf16[32,4096]{1,0:T(8,128)(2,1)}, bf16[32,4096]{1,0:T(8,128)(2,1)}, u32[]{:S(2)}, u32[]{:S(2)}) collective-permute-start(bf16[32,4096]{1,0:T(8,128)(2,1)} %slice.9), channel_id=1, source_target_pairs={{0,6},{2,0},{4,2},{6,4},{1,7},{3,1},{5,3},{7,5},{8,14},{10,8},{12,... | collective-permute-start | bytes 786440 | tf_op jit(solution)/shard_map/ppermute | solution.py:306
  21.2 1.0 %copy-done.4 = bf16[1024,256]{1,0:T(8,128)(2,1)S(1)} copy-done((bf16[1024,256]{1,0:T(8,128)(2,1)S(1)}, bf16[1024,256]{1,0:T(8,128)(2,1)}, u32[]{:S(2)}) %copy-start.4) | copy-done | bytes 524312
  22.2 1.4 %prep_input.1 = bf16[8,256,128]{2,1,0:T(8,128)(2,1)S(1)} custom-call(bf16[1024,256]{1,0:T(8,128)(2,1)S(1)} %copy-done.4), custom_call_target="tpu_custom_call" | custom-call | flops 2000000000 | bytes 1048576 | tf_op jit(solution)/shard_map/prep_input/pallas_call | solution.py:59
  23.6 0.8 copy-done.2
  24.4 5.9 %all-to-all-start.2 = ((bf16[8,256,128]{2,1,0:T(8,128)(2,1)}), bf16[8,256,128]{2,1,0:T(8,128)(2,1)}, u32[]{:S(2)}, u32[]{:S(2)}) async-start(bf16[8,256,128]{2,1,0:T(8,128)(2,1)} %copy-done.2), calls=%async_computation.2 | async-start | bytes 1048576 | tf_op jit(solution)/shard_map/all_to_all | solution.py:304
  30.5 3.2 %collective-permute-start.7 = (bf16[64,4096]{1,0:T(8,128)(2,1)}, bf16[64,4096]{1,0:T(8,128)(2,1)}, u32[]{:S(2)}, u32[]{:S(2)}) collective-permute-start(bf16[64,4096]{1,0:T(8,128)(2,1)} %collective-permute-done.5.refs_0_), channel_id=1, source_target_pairs={{0,6},{2,0},{4,2},{6,4},{1,7},{3,1},{5,3},{7,5},{8,14},{10,8},{12,... | collective-permute-start | bytes 1572872 | tf_op jit(solution)/shard_map/ppermute | solution.py:308
  33.7 4.1 %collective-permute-start.8 = (bf16[32,4096]{1,0:T(8,128)(2,1)S(1)}, bf16[32,4096]{1,0:T(8,128)(2,1)}, u32[]{:S(2)}, u32[]{:S(2)}) collective-permute-start(bf16[32,4096]{1,0:T(8,128)(2,1)S(1)} %collective-permute-done.3.refs_3_), channel_id=1, source_target_pairs={{0,24},{8,16},{16,8},{24,0},{1,25},{9,17},{17,9},{25,1},{2,26},{10... | collective-permute-start | bytes 786440 | tf_op jit(solution)/shard_map/ppermute | solution.py:309
  37.9 1.0 %copy-done.3 = bf16[64,4096]{1,0:T(8,128)(2,1)S(1)} copy-done((bf16[64,4096]{1,0:T(8,128)(2,1)S(1)}, bf16[64,4096]{1,0:T(8,128)(2,1)}, u32[]{:S(2)}) %copy-start.3) | copy-done | bytes 524312
  39.0 5.2 %project.2 = bf16[512,256]{1,0:T(8,128)(2,1)} custom-call(s32[2]{0:T(128)S(1)} %pad_add_fusion.s_ref, bf16[256,4096]{1,0:T(8,128)(2,1)S(1)} %copy-done.1, bf16[256,4096]{1,0:T(8,128)(2,1)} %collective-permute-done.other_ref, bf16[64,4096]{1,0:T(8,128)(2,1)S(1)} %copy-done.3, bf16[64,4096]{1,0:T(8,128)(2,1)S(1)} %collective-permute-done.1.refs_1_, ...), custom_call_target="tpu_custom_call" | custom-call | flops 1073741824 | bytes 6291456 | tf_op jit(solution)/shard_map/project/pallas_call | solution.py:129
  44.1 4.4 %all-to-all-start = ((bf16[16,32,256]{2,1,0:T(8,128)(2,1)}), bf16[16,32,256]{2,1,0:T(8,128)(2,1)S(1)}, u32[]{:S(2)}, u32[]{:S(2)}) async-start(bf16[16,32,256]{2,1,0:T(8,128)(2,1)} %bitcast.3), calls=%async_computation | async-start | bytes 524288 | tf_op jit(solution)/shard_map/all_to_all | solution.py:320
  48.5 5.5 %project.3 = bf16[512,256]{1,0:T(8,128)(2,1)} custom-call(s32[2]{0:T(128)S(1)} %pad_add_fusion.s_ref, bf16[256,4096]{1,0:T(8,128)(2,1)S(1)} %copy-done.1, bf16[256,4096]{1,0:T(8,128)(2,1)} %collective-permute-done.other_ref, bf16[64,4096]{1,0:T(8,128)(2,1)} %collective-permute-done.5.refs_0_, bf16[64,4096]{1,0:T(8,128)(2,1)} %collective-permute-done.6.refs_1_, ...), custom_call_target="tpu_custom_call" | custom-call | flops 1073741824 | bytes 6291456 | tf_op jit(solution)/shard_map/project/pallas_call | solution.py:129
  54.1 2.6 %all-to-all-done.g0_ref = bf16[16,32,256]{2,1,0:T(8,128)(2,1)S(1)} async-done(((bf16[16,32,256]{2,1,0:T(8,128)(2,1)}), bf16[16,32,256]{2,1,0:T(8,128)(2,1)S(1)}, u32[]{:S(2)}, u32[]{:S(2)}) %all-to-all-start) | async-done | bytes 262176 | tf_op jit(solution)/shard_map/all_to_all | solution.py:320
  56.6 3.7 %all-to-all-start.1 = ((bf16[16,32,256]{2,1,0:T(8,128)(2,1)}), bf16[16,32,256]{2,1,0:T(8,128)(2,1)S(1)}, u32[]{:S(2)}, u32[]{:S(2)}) async-start(bf16[16,32,256]{2,1,0:T(8,128)(2,1)} %bitcast.4), calls=%async_computation.1 | async-start | bytes 524288 | tf_op jit(solution)/shard_map/all_to_all | solution.py:325
  60.5 2.5 %toeplitz_tiles.1 = (bf16[65,128,128]{2,1,0:T(8,128)(2,1)S(1)}, bf16[256,1024]{1,0:T(8,128)(2,1)S(1)}) custom-call(bf16[64,128]{1,0:T(8,128)(2,1)S(1)} %bitcast.6, bf16[8,256,128]{2,1,0:T(8,128)(2,1)} %all-to-all-done.2.x_ref), custom_call_target="tpu_custom_call" | custom-call | flops 2000000000 | bytes 2097152 | tf_op jit(solution)/shard_map/toeplitz_tiles/pallas_call | solution.py:86
  63.0 1.3 %copy-done.5 = bf16[65,128,128]{2,1,0:T(8,128)(2,1)} copy-done((bf16[65,128,128]{2,1,0:T(8,128)(2,1)}, bf16[65,128,128]{2,1,0:T(8,128)(2,1)S(1)}, u32[]{:S(2)}) %copy-start.5) | copy-done | bytes 2129944
  64.3 4.0 %all-to-all-done.1.g1_ref = bf16[16,32,256]{2,1,0:T(8,128)(2,1)S(1)} async-done(((bf16[16,32,256]{2,1,0:T(8,128)(2,1)}), bf16[16,32,256]{2,1,0:T(8,128)(2,1)S(1)}, u32[]{:S(2)}, u32[]{:S(2)}) %all-to-all-start.1) | async-done | bytes 262176 | tf_op jit(solution)/shard_map/all_to_all | solution.py:325
  68.3 1.6 %copy-done.6 = bf16[65,128,128]{2,1,0:T(8,128)(2,1)S(1)} copy-done((bf16[65,128,128]{2,1,0:T(8,128)(2,1)S(1)}, bf16[65,128,128]{2,1,0:T(8,128)(2,1)}, u32[]{:S(2)}) %copy-start.6) | copy-done | bytes 2129944
  69.9 6.0 %convolve.1 = bf16[8,40,1024]{2,1,0:T(8,128)(2,1)S(1)} custom-call(s32[1]{0:T(128)} %bitcast.s_ref, bf16[16,32,256]{2,1,0:T(8,128)(2,1)S(1)} %all-to-all-done.g0_ref, bf16[16,32,256]{2,1,0:T(8,128)(2,1)S(1)} %all-to-all-done.1.g1_ref, bf16[256,1024]{1,0:T(8,128)(2,1)S(1)} %get-tuple-element.4.x_ref, bf16[65,128,128]{2,1,0:T(8,128)(2,1)S(1)} %copy-done.6), custom_call_target="tpu_custom_call" | custom-call | flops 6000000000 | bytes 4000000 | tf_op jit(solution)/shard_map/convolve/pallas_call | solution.py:246
  75.9 13.6 %all_to_all.20.m_ref = bf16[8,40,1024]{2,1,0:T(8,128)(2,1)S(1)} all-to-all(bf16[8,40,1024]{2,1,0:T(8,128)(2,1)S(1)} %convolve.1), channel_id=1, replica_groups=mesh['y'=4,'zlo'=2,'zhi'=2,'x'=4,'core'=2] {'y','zlo'}, dimensions={0} | all-to-all | bytes 1310720 | tf_op jit(solution)/shard_map/all_to_all | solution.py:327
  89.5 1.0 %finish.1 = (bf16[1024,256]{1,0:T(8,128)(2,1)}, f32[8,1024]{1,0:T(8,128)}) custom-call(bf16[8,40,1024]{2,1,0:T(8,128)(2,1)S(1)} %all_to_all.20.m_ref), custom_call_target="tpu_custom_call" | custom-call | flops 1000000 | bytes 1310720 | tf_op jit(solution)/shard_map/finish/pallas_call | solution.py:278
  (27 shorter events, 2.3 us)
Async XLA Ops:
  0.6 59.7 %copy-start = (bf16[8,8192]{1,0:T(8,128)(2,1)S(1)}, bf16[8,8192]{1,0:T(8,128)(2,1)}, u32[]{:S(2)}) copy-start(bf16[8,8192]{1,0:T(8,128)(2,1)} %param.7) | copy-start | bytes 393220
  0.6 37.3 %collective-permute-start = (bf16[256,4096]{1,0:T(8,128)(2,1)}, bf16[256,4096]{1,0:T(8,128)(2,1)}, u32[]{:S(2)}, u32[]{:S(2)}) collective-permute-start(bf16[256,4096]{1,0:T(8,128)(2,1)} %own_ref.3), channel_id=1, source_target_pairs={{0,1},{1,0},{2,3},{3,2},{4,5},{5,4},{6,7},{7,6},{8,9},{9,8},{10,11... | collective-permute-start | bytes 6291464 | tf_op jit(solution)/shard_map/ppermute | solution.py:301
  0.7 15.7 %collective-permute-start.1 = (bf16[64,4096]{1,0:T(8,128)(2,1)}, bf16[64,4096]{1,0:T(8,128)(2,1)S(1)}, u32[]{:S(2)}, u32[]{:S(2)}) collective-permute-start(bf16[64,4096]{1,0:T(8,128)(2,1)} %refs_0_.1), channel_id=1, source_target_pairs={{0,2},{2,4},{4,6},{6,0},{1,3},{3,5},{5,7},{7,1},{8,10},{10,12},{12... | collective-permute-start | bytes 1572872 | tf_op jit(solution)/shard_map/ppermute | solution.py:299
  2.4 15.2 %collective-permute-start.2 = (bf16[64,4096]{1,0:T(8,128)(2,1)}, bf16[64,4096]{1,0:T(8,128)(2,1)S(1)}, u32[]{:S(2)}, u32[]{:S(2)}) collective-permute-start(bf16[64,4096]{1,0:T(8,128)(2,1)} %refs_0_.1), channel_id=1, source_target_pairs={{0,6},{2,0},{4,2},{6,4},{1,7},{3,1},{5,3},{7,5},{8,14},{10,8},{12,... | collective-permute-start | bytes 1572872 | tf_op jit(solution)/shard_map/ppermute | solution.py:300
  4.0 26.3 %collective-permute-start.5 = (bf16[64,4096]{1,0:T(8,128)(2,1)}, bf16[64,4096]{1,0:T(8,128)(2,1)}, u32[]{:S(2)}, u32[]{:S(2)}) collective-permute-start(bf16[64,4096]{1,0:T(8,128)(2,1)} %refs_0_.1), channel_id=1, source_target_pairs={{0,24},{8,16},{16,8},{24,0},{1,25},{9,17},{17,9},{25,1},{2,26},{10... | collective-permute-start | bytes 1572872 | tf_op jit(solution)/shard_map/ppermute | solution.py:302
  17.2 16.5 %collective-permute-start.3 = (bf16[32,4096]{1,0:T(8,128)(2,1)}, bf16[32,4096]{1,0:T(8,128)(2,1)S(1)}, u32[]{:S(2)}, u32[]{:S(2)}) collective-permute-start(bf16[32,4096]{1,0:T(8,128)(2,1)} %slice.8), channel_id=1, source_target_pairs={{0,2},{2,4},{4,6},{6,0},{1,3},{3,5},{5,7},{7,1},{8,10},{10,12},{12... | collective-permute-start | bytes 786440 | tf_op jit(solution)/shard_map/ppermute | solution.py:305
  18.3 19.4 %collective-permute-start.4 = (bf16[32,4096]{1,0:T(8,128)(2,1)}, bf16[32,4096]{1,0:T(8,128)(2,1)}, u32[]{:S(2)}, u32[]{:S(2)}) collective-permute-start(bf16[32,4096]{1,0:T(8,128)(2,1)} %slice.9), channel_id=1, source_target_pairs={{0,6},{2,0},{4,2},{6,4},{1,7},{3,1},{5,3},{7,5},{8,14},{10,8},{12,... | collective-permute-start | bytes 786440 | tf_op jit(solution)/shard_map/ppermute | solution.py:306
  21.2 1.0 %copy-start.4 = (bf16[1024,256]{1,0:T(8,128)(2,1)S(1)}, bf16[1024,256]{1,0:T(8,128)(2,1)}, u32[]{:S(2)}) copy-start(bf16[1024,256]{1,0:T(8,128)(2,1)} %x_ref.1) | copy-start | bytes 1572868
  22.2 15.7 %copy-start.1 = (bf16[256,4096]{1,0:T(8,128)(2,1)S(1)}, bf16[256,4096]{1,0:T(8,128)(2,1)}, u32[]{:S(2)}) copy-start(bf16[256,4096]{1,0:T(8,128)(2,1)} %own_ref.3) | copy-start | bytes 6291460
  23.6 0.8 copy-start.2
  24.4 19.7 %all-to-all-start.2 = ((bf16[8,256,128]{2,1,0:T(8,128)(2,1)}), bf16[8,256,128]{2,1,0:T(8,128)(2,1)}, u32[]{:S(2)}, u32[]{:S(2)}) async-start(bf16[8,256,128]{2,1,0:T(8,128)(2,1)} %copy-done.2), calls=%async_computation.2 | async-start | bytes 1048576 | tf_op jit(solution)/shard_map/all_to_all | solution.py:304
  30.4 18.1 %collective-permute-start.6 = (bf16[64,4096]{1,0:T(8,128)(2,1)}, bf16[64,4096]{1,0:T(8,128)(2,1)}, u32[]{:S(2)}, u32[]{:S(2)}) collective-permute-start(bf16[64,4096]{1,0:T(8,128)(2,1)} %collective-permute-done.5.refs_0_), channel_id=1, source_target_pairs={{0,2},{2,4},{4,6},{6,0},{1,3},{3,5},{5,7},{7,1},{8,10},{10,12},{12... | collective-permute-start | bytes 1572872 | tf_op jit(solution)/shard_map/ppermute | solution.py:307
  30.5 18.1 %collective-permute-start.7 = (bf16[64,4096]{1,0:T(8,128)(2,1)}, bf16[64,4096]{1,0:T(8,128)(2,1)}, u32[]{:S(2)}, u32[]{:S(2)}) collective-permute-start(bf16[64,4096]{1,0:T(8,128)(2,1)} %collective-permute-done.5.refs_0_), channel_id=1, source_target_pairs={{0,6},{2,0},{4,2},{6,4},{1,7},{3,1},{5,3},{7,5},{8,14},{10,8},{12,... | collective-permute-start | bytes 1572872 | tf_op jit(solution)/shard_map/ppermute | solution.py:308
  33.7 14.8 %collective-permute-start.8 = (bf16[32,4096]{1,0:T(8,128)(2,1)S(1)}, bf16[32,4096]{1,0:T(8,128)(2,1)}, u32[]{:S(2)}, u32[]{:S(2)}) collective-permute-start(bf16[32,4096]{1,0:T(8,128)(2,1)S(1)} %collective-permute-done.3.refs_3_), channel_id=1, source_target_pairs={{0,24},{8,16},{16,8},{24,0},{1,25},{9,17},{17,9},{25,1},{2,26},{10... | collective-permute-start | bytes 786440 | tf_op jit(solution)/shard_map/ppermute | solution.py:309
  37.8 10.8 %collective-permute-start.9 = (bf16[32,4096]{1,0:T(8,128)(2,1)}, bf16[32,4096]{1,0:T(8,128)(2,1)}, u32[]{:S(2)}, u32[]{:S(2)}) collective-permute-start(bf16[32,4096]{1,0:T(8,128)(2,1)} %collective-permute-done.4.refs_4_), channel_id=1, source_target_pairs={{0,24},{8,16},{16,8},{24,0},{1,25},{9,17},{17,9},{25,1},{2,26},{10... | collective-permute-start | bytes 786440 | tf_op jit(solution)/shard_map/ppermute | solution.py:310
  37.9 1.0 %copy-start.3 = (bf16[64,4096]{1,0:T(8,128)(2,1)S(1)}, bf16[64,4096]{1,0:T(8,128)(2,1)}, u32[]{:S(2)}) copy-start(bf16[64,4096]{1,0:T(8,128)(2,1)} %refs_0_.1) | copy-start | bytes 1572868
  44.1 12.5 %all-to-all-start = ((bf16[16,32,256]{2,1,0:T(8,128)(2,1)}), bf16[16,32,256]{2,1,0:T(8,128)(2,1)S(1)}, u32[]{:S(2)}, u32[]{:S(2)}) async-start(bf16[16,32,256]{2,1,0:T(8,128)(2,1)} %bitcast.3), calls=%async_computation | async-start | bytes 524288 | tf_op jit(solution)/shard_map/all_to_all | solution.py:320
  56.6 11.6 %all-to-all-start.1 = ((bf16[16,32,256]{2,1,0:T(8,128)(2,1)}), bf16[16,32,256]{2,1,0:T(8,128)(2,1)S(1)}, u32[]{:S(2)}, u32[]{:S(2)}) async-start(bf16[16,32,256]{2,1,0:T(8,128)(2,1)} %bitcast.4), calls=%async_computation.1 | async-start | bytes 524288 | tf_op jit(solution)/shard_map/all_to_all | solution.py:325
  62.9 1.3 %copy-start.5 = (bf16[65,128,128]{2,1,0:T(8,128)(2,1)}, bf16[65,128,128]{2,1,0:T(8,128)(2,1)S(1)}, u32[]{:S(2)}) copy-start(bf16[65,128,128]{2,1,0:T(8,128)(2,1)S(1)} %get-tuple-element.5.t_ref) | copy-start | bytes 6389764
  68.3 1.6 %copy-start.6 = (bf16[65,128,128]{2,1,0:T(8,128)(2,1)S(1)}, bf16[65,128,128]{2,1,0:T(8,128)(2,1)}, u32[]{:S(2)}) copy-start(bf16[65,128,128]{2,1,0:T(8,128)(2,1)} %copy-done.5) | copy-start | bytes 6389764

commit v2 on v1

v2 whole, which is shorter than its diff:
```python
import functools

import jax
import jax.numpy as jnp
from jax import lax
from jax.experimental import pallas as pl
from jax.experimental.pallas import tpu as pltpu
from jax.sharding import Mesh
from jax.sharding import PartitionSpec as P

F32 = jnp.float32
BF16 = jnp.bfloat16

TILE = 128
BLK = 256
PART = 16
TAIL = 8
STEP = 1024
VMEM_MIB = 24
X_UP = [(i, (i + 1) % 4) for i in range(4)]
X_DOWN = [(i, (i - 1) % 4) for i in range(4)]
Z_NEAR = [(i, 3 - i) for i in range(4)]
SWAP = [(0, 1), (1, 0)]


def mm(a, b, dims=(((1,), (0,)), ((), ()))):
    return lax.dot_general(a, b, dims, preferred_element_type=F32)


def iota(shape, axis):
    return lax.broadcasted_iota(jnp.int32, shape, axis)


def params():
    return pltpu.CompilerParams(vmem_limit_bytes=VMEM_MIB * 2**20)


def cost(flops, moved):
    return pl.CostEstimate(flops=flops, bytes_accessed=moved, transcendentals=0)


def prep_body(x_ref, o_ref, *, groups, width):
    blocks = x_ref.shape[0] // BLK
    chans = x_ref.shape[1]
    flip = (iota((BLK, BLK), 0) + iota((BLK, BLK), 1) == BLK - 1).astype(BF16)
    turned = [
        mm(flip, x_ref[a * BLK : (a + 1) * BLK, :]).astype(BF16) for a in range(blocks)
    ]
    row = iota((chans, TILE), 0)
    col = iota((chans, TILE), 1)
    for g in range(groups):
        total = jnp.zeros((BLK, TILE), F32)
        for a in range(blocks):
            pick = (row - g * width == col - a * width) & (col // width == a)
            total = total + mm(turned[a], pick.astype(BF16))
        o_ref[g] = total.astype(BF16)


def prep_input(x, groups, width):
    return pl.pallas_call(
        functools.partial(prep_body, groups=groups, width=width),
        out_shape=jax.ShapeDtypeStruct((groups, BLK, TILE), BF16),
        name="prep_input",
        compiler_params=params(),
        cost_estimate=cost(2 * 10**9, 4 * x.size),
    )(x)


def project_body(s_ref, own_ref, other_ref, *refs, shifts, join):
    count = len(shifts)
    blocks, o_ref = refs[:count], refs[count + join]
    weight, rows, acc, sem = refs[count + join + 1 :]
    x = s_ref[0]
    core = s_ref[1]
    chans, depth = own_ref.shape
    size = rows.shape[0] // 4
    moves = [(own_ref, weight, 0), (other_ref, weight, chans)]
    for ref, (shift, at) in zip(blocks, shifts):
        spot = lax.rem(x + shift, 4) * size + at
        moves.append((ref, rows, pl.multiple_of(spot, 32)))
    copies = []
    for k in range(depth // STEP):
        span = pl.ds(k * STEP, STEP)
        for i, (ref, held, spot) in enumerate(moves):
            copy = pltpu.make_async_copy(
                ref.at[:, span], held.at[pl.ds(spot, ref.shape[0]), span], sem.at[k, i]
            )
            copy.start()
            copies.append(copy)
    width = rows.shape[0]
    if join:
        o_ref[:, :width] = refs[count][...]
    dims = (((1,), (1,)), ((), ()))
    for k in range(depth // STEP):
        for copy in copies[k * len(moves) : (k + 1) * len(moves)]:
            copy.wait()
        at = slice(k * STEP, (k + 1) * STEP)
        for half in range(2):
            spot = slice(half * chans, (half + 1) * chans)
            value = mm(weight[spot, at], rows[:, at], dims)
            if k:
                acc[spot, :] += value
            else:
                acc[spot, :] = value
    to = slice(join * width, (join + 1) * width)
    at = pl.multiple_of(core * chans, chans)
    o_ref[pl.ds(at, chans), to] = acc[:chans, :].astype(BF16)
    at = pl.multiple_of((1 - core) * chans, chans)
    o_ref[pl.ds(at, chans), to] = acc[chans:, :].astype(BF16)


def project(spots, own, other, blocks, shifts, first=None):
    chans, depth = own.shape
    rows = sum(b.shape[0] for b in blocks)
    extra = [] if first is None else [first]
    join = len(extra)
    return pl.pallas_call(
        functools.partial(project_body, shifts=shifts, join=join),
        out_shape=jax.ShapeDtypeStruct((2 * chans, (1 + join) * rows), BF16),
        in_specs=[pl.BlockSpec(memory_space=pltpu.SMEM)]
        + [pl.BlockSpec(memory_space=pl.ANY)] * (2 + len(blocks))
        + [pl.BlockSpec(memory_space=pltpu.VMEM)] * join,
        scratch_shapes=[
            pltpu.VMEM((2 * chans, depth), BF16),
            pltpu.VMEM((rows, depth), BF16),
            pltpu.VMEM((2 * chans, rows), F32),
            pltpu.SemaphoreType.DMA((depth // STEP, 2 + len(blocks))),
        ],
        name="project",
        compiler_params=params(),
        cost_estimate=cost(4 * chans * rows * depth, 2 * depth * (2 * chans + rows)),
    )(spots, own, other, *blocks, *extra)


def conv_body(s_ref, g_ref, x_ref, f_ref, o_ref, gb, acc, corr, t_ref):
    zhi = s_ref[0]
    width = g_ref.shape[1]
    senders = g_ref.shape[0] // 2
    nb = 4 * senders
    top = nb * width
    lane = iota((width, TILE), 1)
    gb[top:, :] = jnp.zeros((gb.shape[0] - top, BLK), BF16)
    for half in range(2):
        for s in range(senders):
            owner = s ^ half
            zz = 1 - zhi if half else zhi
            for xh in range(2):
                lo = (half * 2 + xh) * TILE
                a = g_ref[s, :, lo : lo + TILE].astype(F32)
                b = g_ref[senders + s, :, lo : lo + TILE].astype(F32)
                left = jnp.where(lane < 64, a, pltpu.roll(b, 64, 1))
                right = jnp.where(lane < 64, pltpu.roll(a, 64, 1), b)
                spot = (owner * 4 + zz * 2 + xh) * width
                at = pl.ds(pl.multiple_of(spot, width), width)
                gb[at, :TILE] = left.astype(BF16)
                gb[at, TILE:] = right.astype(BF16)

    def put(k, value, fresh=False):
        for part in range(TILE // PART):
            piece = value[part * PART : (part + 1) * PART, :]
            at = slice(k * PART, (k + 1) * PART)
            if fresh:
                corr[part, at, :] = piece
            else:
                corr[part, at, :] += piece

    flip = (iota((TILE, TILE), 0) + iota((TILE, TILE), 1) == TILE - 1).astype(BF16)
    turned = mm(f_ref[...], flip)
    t_ref[0] = jnp.zeros((TILE, TILE), BF16)

    def make_tile(k):
        before = turned[k - 1 : k] if k else jnp.zeros((1, TILE), F32)
        line = jnp.concatenate([before, turned[k : k + 1]], axis=1)
        spread = jnp.broadcast_to(line, (TILE, 2 * TILE))
        turn = pltpu.roll(spread, 1, 1, stride=1, stride_axis=0)
        t_ref[k + 1] = turn[:, :TILE].astype(BF16)

    full_x = jnp.concatenate([x_ref[s] for s in range(senders)], axis=1)
    for d in range(nb):
        make_tile(2 * d)
        make_tile(2 * d + 1)
        span = -(-(nb - d) * width // BLK) * BLK
        moved = gb[d * width : d * width + span, :]
        mid = t_ref[2 * d + 1]
        up = t_ref[2 * d + 2]
        down = t_ref[2 * d]
        tile = jnp.concatenate(
            [
                jnp.concatenate([mid, down], axis=1),
                jnp.concatenate([up, mid], axis=1),
            ],
            axis=0,
        )
        if d == 0:
            acc[...] = mm(moved, tile)
        else:
            acc[:span, :] += mm(moved, tile)
        prod = mm(full_x[:, :span], moved)
        put(2 * d, prod[:TILE, :TILE], fresh=d == 0)
        put(2 * d + 1, prod[:TILE, TILE:] + prod[TILE:, :TILE], fresh=True)
        put(2 * d + 2, prod[TILE:, TILE:], fresh=True)

    for s in range(senders):
        for k in range(8):
            a = (s * 4 + k // 2) * width
            lo = k % 2 * TILE
            o_ref[s, k * width : (k + 1) * width, :] = acc[
                a : a + width, lo : lo + TILE
            ].astype(BF16)

    lane = iota((PART, TILE), 1)
    turned = lane <= iota((PART, TILE), 0)
    spill = jnp.zeros((PART, TILE), F32)
    carry = jnp.zeros((1, TILE), F32)
    lines = []
    for k in range(2 * nb + 2):
        total = spill
        if k <= 2 * nb:
            low = corr[0, k * PART : (k + 1) * PART, :]
            spill = jnp.zeros((PART, TILE), F32)
            for part in range(1, TILE // PART):
                by = part * PART
                move = pltpu.roll(corr[part, k * PART : (k + 1) * PART, :], by, 1)
                low = low + jnp.where(lane >= by, move, 0.0)
                spill = spill + jnp.where(lane < by, move, 0.0)
            total = total + low
        move = pltpu.roll(total, 1, 1, stride=1, stride_axis=0)
        line = jnp.sum(jnp.where(turned, 0.0, move), axis=0, keepdims=True)
        if k >= 2:
            lines.append(line + carry)
        carry = jnp.sum(jnp.where(turned, move, 0.0), axis=0, keepdims=True)

    at = 8 * width
    for s in range(senders):
        full = jnp.concatenate(lines[s * TAIL : (s + 1) * TAIL], axis=0)
        first = full.astype(BF16)
        rest = full - first.astype(F32)
        second = rest.astype(BF16)
        third = (rest - second.astype(F32)).astype(BF16)
        o_ref[s, at : at + 2 * TAIL, :] = jnp.concatenate([first, second], axis=0)
        o_ref[s, at + 2 * TAIL :, :] = third


def convolve(spot, g, xt, taps):
    senders = g.shape[0] // 2
    width = g.shape[1]
    nb = 4 * senders
    top = nb * width
    return pl.pallas_call(
        conv_body,
        out_shape=jax.ShapeDtypeStruct((senders, 8 * width + 3 * TAIL, TILE), BF16),
        in_specs=[pl.BlockSpec(memory_space=pltpu.SMEM)]
        + [pl.BlockSpec(memory_space=pltpu.VMEM)] * 3,
        scratch_shapes=[
            pltpu.VMEM((top + BLK, BLK), BF16),
            pltpu.VMEM((top, BLK), F32),
            pltpu.VMEM((TILE // PART, (2 * nb + 1) * PART, TILE), F32),
            pltpu.VMEM((2 * nb + 1, TILE, TILE), BF16),
        ],
        name="convolve",
        compiler_params=params(),
        cost_estimate=cost(6 * 10**9, 4 * 10**6),
    )(spot, g, xt, taps)


def finish_body(m_ref, o_ref, f_ref):
    groups, rows, _ = m_ref.shape
    width = (rows - 3 * TAIL) // 8
    for k in range(8):
        at = slice(k * width, (k + 1) * width)
        for h in range(groups // 4):
            four = [m_ref[4 * h + i, at, :].astype(F32) for i in range(4)]
            flat = jnp.concatenate(four, axis=0)
            o_ref[k * TILE : (k + 1) * TILE, h * TILE : (h + 1) * TILE] = flat.T.astype(BF16)
    at = 8 * width
    for g in range(groups):
        both = m_ref[g, at : at + 2 * TAIL, :].astype(F32)
        total = both[:TAIL] + both[TAIL:] + m_ref[g, at + 2 * TAIL :, :].astype(F32)
        for j in range(TAIL):
            f_ref[g : g + 1, j * TILE : (j + 1) * TILE] = total[j : j + 1, :]


def finish(major):
    groups, rows, lanes = major.shape
    width = (rows - 3 * TAIL) // 8
    return pl.pallas_call(
        finish_body,
        out_shape=(
            jax.ShapeDtypeStruct((8 * lanes, groups * width), BF16),
            jax.ShapeDtypeStruct((groups, TAIL * lanes), F32),
        ),
        name="finish",
        compiler_params=params(),
        cost_estimate=cost(10**6, 4 * major.size),
    )(major)


def on_device(conv_input, grad_out, out_weight, filters):
    groups = filters.shape[0]
    width = conv_input.shape[1] // groups
    seq = ("y", "zlo")
    near = ("zlo", "zhi")
    x = lax.axis_index("x").astype(jnp.int32)
    core = lax.axis_index("core").astype(jnp.int32)
    zhi = lax.axis_index("zhi").astype(jnp.int32)
    half = grad_out.shape[0] // 2
    before = lax.ppermute(grad_out, "x", X_UP)
    after = lax.ppermute(grad_out, "x", X_DOWN)
    near_own = lax.ppermute(grad_out, near, Z_NEAR)
    other_weight = lax.ppermute(out_weight, "core", SWAP)
    far_a = lax.ppermute(before[:half], "x", X_UP)
    far_b = lax.ppermute(after[half:], "x", X_DOWN)
    turned = prep_input(conv_input, groups, width)
    turned = lax.all_to_all(turned, seq, 0, 0, tiled=True)
    near_before = lax.ppermute(near_own, "x", X_UP)
    near_after = lax.ppermute(near_own, "x", X_DOWN)
    near_far_a = lax.ppermute(far_a, near, Z_NEAR)
    near_far_b = lax.ppermute(far_b, near, Z_NEAR)
    taps = lax.dynamic_index_in_dim(filters, lax.axis_index(seq), 0, False)
    taps = taps.reshape(-1, TILE)
    spots = jnp.stack([x, core])
    shifts = [(0, 0), (3, 0), (1, 0), (2, 0), (2, half)]
    g = project(
        spots, out_weight, other_weight,
        [grad_out, before, after, far_a, far_b], shifts,
    )
    g = project(
        spots, out_weight, other_weight,
        [near_own, near_before, near_after, near_far_a, near_far_b], shifts, g,
    )
    g = g.reshape(2 * groups, width, -1)
    g = lax.all_to_all(g, ("core",) + seq, 0, 0, tiled=True)
    major = convolve(zhi.reshape(1), g, turned, taps)
    major = lax.all_to_all(major, seq, 0, 0, tiled=True)
    return finish(major)


def solution(mesh):
    fine = Mesh(
        mesh.devices.reshape(4, 2, 2, 4, 2),
        ("y", "zlo", "zhi", "x", "core"),
        axis_types=(jax.sharding.AxisType.Auto,) * 5,
    )
    seq = ("y", "zlo")
    chan = ("zhi", "x", "core")
    in_specs = (P(seq, chan), P(seq + chan, None), P(chan, None), P(chan, None))
    out_specs = (P(seq, chan), P(chan, seq))
    return jax.shard_map(
        on_device, mesh=fine, in_specs=in_specs, out_specs=out_specs, check_vma=False
    )
```

time: 91.2 us -> 88.8 us (0.974)
  waiting for transfers between devices: 14.9 us -> 25 us
  Pallas kernels: 21.5 us -> 17.4 us
  local copies, waits for them, and re-layouts: 7.38 us -> 3.74 us
  starting transfers between devices: 32.2 us -> 28.6 us
    all_to_all x2 -> x1, waiting for transfers between devices: 6.56 us -> 11 us  [on_device(): g = lax.all_to_all(g, ('core',) + seq, 0, 0, tiled=True)]
    pallas_call x5 -> x4, Pallas kernels: 20.1 us -> 16 us  [the longest x2 7.86 us: project(): pl.pallas_call(functools.partial(project_body, shifts=shifts, join=join),...]
    all_to_all x2 -> x1, starting transfers between devices: 8.06 us -> 4.37 us  [on_device(): g = lax.all_to_all(g, ('core',) + seq, 0, 0, tiled=True)]
    ppermute x1, waiting for transfers between devices: 0.01 us -> 3.02 us  [on_device(): near_far_b = lax.ppermute(far_b, near, Z_NEAR)]
    unnamed x14 -> x10, local copies, waits for them, and re-layouts: 5.81 us -> 2.89 us
    ppermute x1, waiting for transfers between devices: 0.01 us -> 2.66 us  [on_device(): near_far_a = lax.ppermute(far_a, near, Z_NEAR)]
  transfers between devices with their start and end apart: 13 -> 12, of which waited for: 3 -> 4; matrix products, arithmetic and copies ran while one was open for 2% -> 1% of each run, Pallas kernels for 16% -> 10%
where the time goes in v2:
time: 88.8 us; the launch traced here: 88.3 us
  starting transfers between devices  28.6 us (32%)
  waiting for transfers between devices  25 us (28%)
  Pallas kernels  17.4 us (20%)
  blocking collectives  12.8 us (14%)
  local copies, waits for them, and re-layouts  3.74 us (4%)
    all_to_all x1, blocking collectives, on_device(): major = lax.all_to_all(major, seq, 0, 0, tiled=True)  12.8 us
    all_to_all x1, waiting for transfers between devices, on_device(): g = lax.all_to_all(g, ('core',) + seq, 0, 0, tiled=True)  11 us
    ppermute x1, waiting for transfers between devices, on_device(): before = lax.ppermute(grad_out, 'x', X_UP)  8.29 us
    pallas_call x2, Pallas kernels, project(): pl.pallas_call(functools.partial(project_body, shifts=shifts, join=join),...  7.86 us
    pallas_call x1, Pallas kernels, convolve(): pl.pallas_call(conv_body, out_shape=jax.ShapeDtypeStruct((senders, 8 * wi...  7.09 us
    all_to_all x1, starting transfers between devices, on_device(): turned = lax.all_to_all(turned, seq, 0, 0, tiled=True)  5.94 us
    all_to_all x1, starting transfers between devices, on_device(): g = lax.all_to_all(g, ('core',) + seq, 0, 0, tiled=True)  4.37 us
    ppermute x1, starting transfers between devices, on_device(): near_own = lax.ppermute(grad_out, near, Z_NEAR)  4.15 us
  transfers between devices with their start and end apart: 12, of which 4 were waited for; matrix products, arithmetic and copies ran while one was open for 1% of the time, Pallas kernels for 10%

profile of v2, /device:TPU:0, one launch (start us, length us, event | category | flops | bytes accessed | tf_op | source)
XLA Modules:
  0.0 88.3 jit_solution(8266594497957699301)
XLA Ops:
  0.7 1.7 %collective-permute-start.4 = (bf16[64,4096]{1,0:T(8,128)(2,1)}, bf16[64,4096]{1,0:T(8,128)(2,1)S(1)}, u32[]{:S(2)}, u32[]{:S(2)}) collective-permute-start(bf16[64,4096]{1,0:T(8,128)(2,1)} %refs_0_.1), channel_id=1, source_target_pairs={{0,2},{2,4},{4,6},{6,0},{1,3},{3,5},{5,7},{7,1},{8,10},{10,12},{12... | collective-permute-start | bytes 1572872 | tf_op jit(solution)/shard_map/ppermute | solution.py:307
  2.4 1.6 %collective-permute-start.7 = (bf16[64,4096]{1,0:T(8,128)(2,1)}, bf16[64,4096]{1,0:T(8,128)(2,1)S(1)}, u32[]{:S(2)}, u32[]{:S(2)}) collective-permute-start(bf16[64,4096]{1,0:T(8,128)(2,1)} %refs_0_.1), channel_id=1, source_target_pairs={{0,6},{2,0},{4,2},{6,4},{1,7},{3,1},{5,3},{7,5},{8,14},{10,8},{12,... | collective-permute-start | bytes 1572872 | tf_op jit(solution)/shard_map/ppermute | solution.py:308
  4.0 4.1 %collective-permute-start.1 = (bf16[64,4096]{1,0:T(8,128)(2,1)}, bf16[64,4096]{1,0:T(8,128)(2,1)}, u32[]{:S(2)}, u32[]{:S(2)}) collective-permute-start(bf16[64,4096]{1,0:T(8,128)(2,1)} %refs_0_.1), channel_id=1, source_target_pairs={{0,24},{8,16},{16,8},{24,0},{1,25},{9,17},{17,9},{25,1},{2,26},{10... | collective-permute-start | bytes 1572872 | tf_op jit(solution)/shard_map/ppermute | solution.py:309
  8.2 8.3 %collective-permute-done.4.refs_1_ = bf16[64,4096]{1,0:T(8,128)(2,1)S(1)} collective-permute-done((bf16[64,4096]{1,0:T(8,128)(2,1)}, bf16[64,4096]{1,0:T(8,128)(2,1)S(1)}, u32[]{:S(2)}, u32[]{:S(2)}) %collective-permute-start.4) | collective-permute-done | bytes 524320 | tf_op jit(solution)/shard_map/ppermute | solution.py:307
  16.5 0.5 collective-permute-start.5
  17.0 0.7 slice.9
  17.7 2.8 %collective-permute-start.8 = (bf16[32,4096]{1,0:T(8,128)(2,1)}, bf16[32,4096]{1,0:T(8,128)(2,1)}, u32[]{:S(2)}, u32[]{:S(2)}) collective-permute-start(bf16[32,4096]{1,0:T(8,128)(2,1)} %slice.9), channel_id=1, source_target_pairs={{0,6},{2,0},{4,2},{6,4},{1,7},{3,1},{5,3},{7,5},{8,14},{10,8},{12,... | collective-permute-start | bytes 786440 | tf_op jit(solution)/shard_map/ppermute | solution.py:312
  20.5 0.2 collective-permute-start.2
  20.8 3.0 %collective-permute-start.3 = (bf16[64,4096]{1,0:T(8,128)(2,1)}, bf16[64,4096]{1,0:T(8,128)(2,1)}, u32[]{:S(2)}, u32[]{:S(2)}) collective-permute-start(bf16[64,4096]{1,0:T(8,128)(2,1)} %collective-permute-done.1.refs_0_), channel_id=1, source_target_pairs={{0,6},{2,0},{4,2},{6,4},{1,7},{3,1},{5,3},{7,5},{8,14},{10,8},{12,... | collective-permute-start | bytes 1572872 | tf_op jit(solution)/shard_map/ppermute | solution.py:316
  23.8 1.0 %copy-done.4 = bf16[1024,256]{1,0:T(8,128)(2,1)S(1)} copy-done((bf16[1024,256]{1,0:T(8,128)(2,1)S(1)}, bf16[1024,256]{1,0:T(8,128)(2,1)}, u32[]{:S(2)}) %copy-start.4) | copy-done | bytes 524312
  24.8 1.4 %prep_input.1 = bf16[8,256,128]{2,1,0:T(8,128)(2,1)S(1)} custom-call(bf16[1024,256]{1,0:T(8,128)(2,1)S(1)} %copy-done.4), custom_call_target="tpu_custom_call" | custom-call | flops 2000000000 | bytes 1048576 | tf_op jit(solution)/shard_map/prep_input/pallas_call | solution.py:60
  26.2 0.8 copy-done.2
  27.0 5.9 %all-to-all-start.1 = ((bf16[8,256,128]{2,1,0:T(8,128)(2,1)}), bf16[8,256,128]{2,1,0:T(8,128)(2,1)}, u32[]{:S(2)}, u32[]{:S(2)}) async-start(bf16[8,256,128]{2,1,0:T(8,128)(2,1)} %copy-done.2), calls=%async_computation.1 | async-start | bytes 1048576 | tf_op jit(solution)/shard_map/all_to_all | solution.py:314
  33.0 4.1 %collective-permute-start.6 = (bf16[32,4096]{1,0:T(8,128)(2,1)}, bf16[32,4096]{1,0:T(8,128)(2,1)S(1)}, u32[]{:S(2)}, u32[]{:S(2)}) collective-permute-start(bf16[32,4096]{1,0:T(8,128)(2,1)} %collective-permute-done.5.refs_3_), channel_id=1, source_target_pairs={{0,24},{8,16},{16,8},{24,0},{1,25},{9,17},{17,9},{25,1},{2,26},{10... | collective-permute-start | bytes 786440 | tf_op jit(solution)/shard_map/ppermute | solution.py:317
  37.3 1.0 %copy-done.3 = bf16[64,4096]{1,0:T(8,128)(2,1)S(1)} copy-done((bf16[64,4096]{1,0:T(8,128)(2,1)S(1)}, bf16[64,4096]{1,0:T(8,128)(2,1)}, u32[]{:S(2)}) %copy-start.3) | copy-done | bytes 524312
  38.3 3.5 %project.2.refs_5_ = bf16[512,256]{1,0:T(8,128)(2,1)S(1)} custom-call(s32[2]{0:T(128)S(1)} %pad_add_fusion.s_ref, bf16[256,4096]{1,0:T(8,128)(2,1)S(1)} %copy-done.1, bf16[256,4096]{1,0:T(8,128)(2,1)} %collective-permute-done.other_ref, bf16[64,4096]{1,0:T(8,128)(2,1)S(1)} %copy-done.3, bf16[64,4096]{1,0:T(8,128)(2,1)S(1)} %collective-permute-done.4.refs_1_, ...), custom_call_target="tpu_custom_call" | custom-call | flops 1073741824 | bytes 6291456 | tf_op jit(solution)/shard_map/project/pallas_call | solution.py:117
  41.8 2.7 %collective-permute-done.6.refs_3_ = bf16[32,4096]{1,0:T(8,128)(2,1)S(1)} collective-permute-done((bf16[32,4096]{1,0:T(8,128)(2,1)}, bf16[32,4096]{1,0:T(8,128)(2,1)S(1)}, u32[]{:S(2)}, u32[]{:S(2)}) %collective-permute-start.6) | collective-permute-done | bytes 262176 | tf_op jit(solution)/shard_map/ppermute | solution.py:317
  44.5 3.0 %collective-permute-done.9.refs_4_ = bf16[32,4096]{1,0:T(8,128)(2,1)} collective-permute-done((bf16[32,4096]{1,0:T(8,128)(2,1)}, bf16[32,4096]{1,0:T(8,128)(2,1)}, u32[]{:S(2)}, u32[]{:S(2)}) %collective-permute-start.9) | collective-permute-done | bytes 262176 | tf_op jit(solution)/shard_map/ppermute | solution.py:318
  47.5 4.4 %project.3 = bf16[512,512]{1,0:T(8,128)(2,1)} custom-call(s32[2]{0:T(128)S(1)} %pad_add_fusion.s_ref, bf16[256,4096]{1,0:T(8,128)(2,1)S(1)} %copy-done.1, bf16[256,4096]{1,0:T(8,128)(2,1)} %collective-permute-done.other_ref, bf16[64,4096]{1,0:T(8,128)(2,1)} %collective-permute-done.1.refs_0_, bf16[64,4096]{1,0:T(8,128)(2,1)} %collective-permute-done.2.refs_1_, ...), custom_call_target="tpu_custom_call" | custom-call | flops 1073741824 | bytes 6291456 | tf_op jit(solution)/shard_map/project/pallas_call | solution.py:117
  51.9 4.4 %all-to-all-start = ((bf16[16,32,512]{2,1,0:T(8,128)(2,1)}), bf16[16,32,512]{2,1,0:T(8,128)(2,1)S(1)}, u32[]{:S(2)}, u32[]{:S(2)}) async-start(bf16[16,32,512]{2,1,0:T(8,128)(2,1)} %bitcast.3), calls=%async_computation | async-start | bytes 1048576 | tf_op jit(solution)/shard_map/all_to_all | solution.py:332
  56.4 11.0 %all-to-all-done.g_ref = bf16[16,32,512]{2,1,0:T(8,128)(2,1)S(1)} async-done(((bf16[16,32,512]{2,1,0:T(8,128)(2,1)}), bf16[16,32,512]{2,1,0:T(8,128)(2,1)S(1)}, u32[]{:S(2)}, u32[]{:S(2)}) %all-to-all-start) | async-done | bytes 524320 | tf_op jit(solution)/shard_map/all_to_all | solution.py:332
  67.4 7.1 %convolve.1 = bf16[8,280,128]{2,1,0:T(8,128)(2,1)S(1)} custom-call(s32[1]{0:T(128)} %bitcast.s_ref, bf16[16,32,512]{2,1,0:T(8,128)(2,1)S(1)} %all-to-all-done.g_ref, bf16[8,256,128]{2,1,0:T(8,128)(2,1)} %all-to-all-done.1.x_ref, bf16[64,128]{1,0:T(8,128)(2,1)S(1)} %bitcast.5), custom_call_target="tpu_custom_call" | custom-call | flops 6000000000 | bytes 4000000 | tf_op jit(solution)/shard_map/convolve/pallas_call | solution.py:249
  74.5 12.8 %all_to_all.15.m_ref = bf16[8,280,128]{2,1,0:T(8,128)(2,1)S(1)} all-to-all(bf16[8,280,128]{2,1,0:T(8,128)(2,1)S(1)} %convolve.1), channel_id=1, replica_groups=mesh['y'=4,'zlo'=2,'zhi'=2,'x'=4,'core'=2] {'y','zlo'}, dimensions={0} | all-to-all | bytes 1146880 | tf_op jit(solution)/shard_map/all_to_all | solution.py:334
  87.3 1.0 %finish.1 = (bf16[1024,256]{1,0:T(8,128)(2,1)}, f32[8,1024]{1,0:T(8,128)}) custom-call(bf16[8,280,128]{2,1,0:T(8,128)(2,1)S(1)} %all_to_all.15.m_ref), custom_call_target="tpu_custom_call" | custom-call | flops 1000000 | bytes 1146880 | tf_op jit(solution)/shard_map/finish/pallas_call | solution.py:286
  (20 shorter events, 0.4 us)
Async XLA Ops:
  0.6 55.7 %copy-start = (bf16[8,8192]{1,0:T(8,128)(2,1)S(1)}, bf16[8,8192]{1,0:T(8,128)(2,1)}, u32[]{:S(2)}) copy-start(bf16[8,8192]{1,0:T(8,128)(2,1)} %param.7) | copy-start | bytes 393220
  0.6 36.6 %collective-permute-start = (bf16[256,4096]{1,0:T(8,128)(2,1)}, bf16[256,4096]{1,0:T(8,128)(2,1)}, u32[]{:S(2)}, u32[]{:S(2)}) collective-permute-start(bf16[256,4096]{1,0:T(8,128)(2,1)} %own_ref.3), channel_id=1, source_target_pairs={{0,1},{1,0},{2,3},{3,2},{4,5},{5,4},{6,7},{7,6},{8,9},{9,8},{10,11... | collective-permute-start | bytes 6291464 | tf_op jit(solution)/shard_map/ppermute | solution.py:310
  0.7 15.7 %collective-permute-start.4 = (bf16[64,4096]{1,0:T(8,128)(2,1)}, bf16[64,4096]{1,0:T(8,128)(2,1)S(1)}, u32[]{:S(2)}, u32[]{:S(2)}) collective-permute-start(bf16[64,4096]{1,0:T(8,128)(2,1)} %refs_0_.1), channel_id=1, source_target_pairs={{0,2},{2,4},{4,6},{6,0},{1,3},{3,5},{5,7},{7,1},{8,10},{10,12},{12... | collective-permute-start | bytes 1572872 | tf_op jit(solution)/shard_map/ppermute | solution.py:307
  2.4 14.6 %collective-permute-start.7 = (bf16[64,4096]{1,0:T(8,128)(2,1)}, bf16[64,4096]{1,0:T(8,128)(2,1)S(1)}, u32[]{:S(2)}, u32[]{:S(2)}) collective-permute-start(bf16[64,4096]{1,0:T(8,128)(2,1)} %refs_0_.1), channel_id=1, source_target_pairs={{0,6},{2,0},{4,2},{6,4},{1,7},{3,1},{5,3},{7,5},{8,14},{10,8},{12,... | collective-permute-start | bytes 1572872 | tf_op jit(solution)/shard_map/ppermute | solution.py:308
  4.0 16.5 %collective-permute-start.1 = (bf16[64,4096]{1,0:T(8,128)(2,1)}, bf16[64,4096]{1,0:T(8,128)(2,1)}, u32[]{:S(2)}, u32[]{:S(2)}) collective-permute-start(bf16[64,4096]{1,0:T(8,128)(2,1)} %refs_0_.1), channel_id=1, source_target_pairs={{0,24},{8,16},{16,8},{24,0},{1,25},{9,17},{17,9},{25,1},{2,26},{10... | collective-permute-start | bytes 1572872 | tf_op jit(solution)/shard_map/ppermute | solution.py:309
  16.5 16.5 %collective-permute-start.5 = (bf16[32,4096]{1,0:T(8,128)(2,1)S(1)}, bf16[32,4096]{1,0:T(8,128)(2,1)}, u32[]{:S(2)}, u32[]{:S(2)}) collective-permute-start(bf16[32,4096]{1,0:T(8,128)(2,1)S(1)} %slice.8), channel_id=1, source_target_pairs={{0,2},{2,4},{4,6},{6,0},{1,3},{3,5},{5,7},{7,1},{8,10},{10,12},{12... | collective-permute-start | bytes 786440 | tf_op jit(solution)/shard_map/ppermute | solution.py:311
  17.7 19.4 %collective-permute-start.8 = (bf16[32,4096]{1,0:T(8,128)(2,1)}, bf16[32,4096]{1,0:T(8,128)(2,1)}, u32[]{:S(2)}, u32[]{:S(2)}) collective-permute-start(bf16[32,4096]{1,0:T(8,128)(2,1)} %slice.9), channel_id=1, source_target_pairs={{0,6},{2,0},{4,2},{6,4},{1,7},{3,1},{5,3},{7,5},{8,14},{10,8},{12,... | collective-permute-start | bytes 786440 | tf_op jit(solution)/shard_map/ppermute | solution.py:312
  20.5 27.0 %collective-permute-start.2 = (bf16[64,4096]{1,0:T(8,128)(2,1)}, bf16[64,4096]{1,0:T(8,128)(2,1)}, u32[]{:S(2)}, u32[]{:S(2)}) collective-permute-start(bf16[64,4096]{1,0:T(8,128)(2,1)} %collective-permute-done.1.refs_0_), channel_id=1, source_target_pairs={{0,2},{2,4},{4,6},{6,0},{1,3},{3,5},{5,7},{7,1},{8,10},{10,12},{12... | collective-permute-start | bytes 1572872 | tf_op jit(solution)/shard_map/ppermute | solution.py:315
  20.8 26.7 %collective-permute-start.3 = (bf16[64,4096]{1,0:T(8,128)(2,1)}, bf16[64,4096]{1,0:T(8,128)(2,1)}, u32[]{:S(2)}, u32[]{:S(2)}) collective-permute-start(bf16[64,4096]{1,0:T(8,128)(2,1)} %collective-permute-done.1.refs_0_), channel_id=1, source_target_pairs={{0,6},{2,0},{4,2},{6,4},{1,7},{3,1},{5,3},{7,5},{8,14},{10,8},{12,... | collective-permute-start | bytes 1572872 | tf_op jit(solution)/shard_map/ppermute | solution.py:316
  23.8 1.0 %copy-start.4 = (bf16[1024,256]{1,0:T(8,128)(2,1)S(1)}, bf16[1024,256]{1,0:T(8,128)(2,1)}, u32[]{:S(2)}) copy-start(bf16[1024,256]{1,0:T(8,128)(2,1)} %x_ref.1) | copy-start | bytes 1572868
  24.8 12.5 %copy-start.1 = (bf16[256,4096]{1,0:T(8,128)(2,1)S(1)}, bf16[256,4096]{1,0:T(8,128)(2,1)}, u32[]{:S(2)}) copy-start(bf16[256,4096]{1,0:T(8,128)(2,1)} %own_ref.3) | copy-start | bytes 6291460
  26.2 0.8 copy-start.2
  27.0 24.9 %all-to-all-start.1 = ((bf16[8,256,128]{2,1,0:T(8,128)(2,1)}), bf16[8,256,128]{2,1,0:T(8,128)(2,1)}, u32[]{:S(2)}, u32[]{:S(2)}) async-start(bf16[8,256,128]{2,1,0:T(8,128)(2,1)} %copy-done.2), calls=%async_computation.1 | async-start | bytes 1048576 | tf_op jit(solution)/shard_map/all_to_all | solution.py:314
  33.0 11.5 %collective-permute-start.6 = (bf16[32,4096]{1,0:T(8,128)(2,1)}, bf16[32,4096]{1,0:T(8,128)(2,1)S(1)}, u32[]{:S(2)}, u32[]{:S(2)}) collective-permute-start(bf16[32,4096]{1,0:T(8,128)(2,1)} %collective-permute-done.5.refs_3_), channel_id=1, source_target_pairs={{0,24},{8,16},{16,8},{24,0},{1,25},{9,17},{17,9},{25,1},{2,26},{10... | collective-permute-start | bytes 786440 | tf_op jit(solution)/shard_map/ppermute | solution.py:317
  37.1 10.4 %collective-permute-start.9 = (bf16[32,4096]{1,0:T(8,128)(2,1)}, bf16[32,4096]{1,0:T(8,128)(2,1)}, u32[]{:S(2)}, u32[]{:S(2)}) collective-permute-start(bf16[32,4096]{1,0:T(8,128)(2,1)} %collective-permute-done.8.refs_4_), channel_id=1, source_target_pairs={{0,24},{8,16},{16,8},{24,0},{1,25},{9,17},{17,9},{25,1},{2,26},{10... | collective-permute-start | bytes 786440 | tf_op jit(solution)/shard_map/ppermute | solution.py:318
  37.3 1.0 %copy-start.3 = (bf16[64,4096]{1,0:T(8,128)(2,1)S(1)}, bf16[64,4096]{1,0:T(8,128)(2,1)}, u32[]{:S(2)}) copy-start(bf16[64,4096]{1,0:T(8,128)(2,1)} %refs_0_.1) | copy-start | bytes 1572868
  51.9 15.5 %all-to-all-start = ((bf16[16,32,512]{2,1,0:T(8,128)(2,1)}), bf16[16,32,512]{2,1,0:T(8,128)(2,1)S(1)}, u32[]{:S(2)}, u32[]{:S(2)}) async-start(bf16[16,32,512]{2,1,0:T(8,128)(2,1)} %bitcast.3), calls=%async_computation | async-start | bytes 1048576 | tf_op jit(solution)/shard_map/all_to_all | solution.py:332

commit v3 on v2

--- a/solution.py
+++ b/solution.py
@@ -16,6 +16,7 @@
 PART = 16
 TAIL = 8
 STEP = 1024
+EARLY = 56
 VMEM_MIB = 24
 X_UP = [(i, (i + 1) % 4) for i in range(4)]
 X_DOWN = [(i, (i - 1) % 4) for i in range(4)]
@@ -66,74 +67,127 @@
     )(x)
 
 
-def project_body(s_ref, own_ref, other_ref, *refs, shifts, join):
-    count = len(shifts)
-    blocks, o_ref = refs[:count], refs[count + join]
-    weight, rows, acc, sem = refs[count + join + 1 :]
+def turn_taps(f_ref):
+    flip = (iota((TILE, TILE), 0) + iota((TILE, TILE), 1) == TILE - 1).astype(BF16)
+    return mm(f_ref[...], flip)
+
+
+def toeplitz_tile(turned, k):
+    before = turned[k - 1 : k] if k else jnp.zeros((1, TILE), F32)
+    line = jnp.concatenate([before, turned[k : k + 1]], axis=1)
+    spread = jnp.broadcast_to(line, (TILE, 2 * TILE))
+    turn = pltpu.roll(spread, 1, 1, stride=1, stride_axis=0)
+    return turn[:, :TILE].astype(BF16)
+
+
+def ready_body(f_ref, x_ref, t_ref, y_ref):
+    for s in range(x_ref.shape[0]):
+        y_ref[:, s * TILE : (s + 1) * TILE] = x_ref[s]
+    turned = turn_taps(f_ref)
+    t_ref[0] = jnp.zeros((TILE, TILE), BF16)
+    for k in range(t_ref.shape[0] - 1):
+        t_ref[k + 1] = toeplitz_tile(turned, k)
+
+
+def ready(taps, x):
+    vmem = pl.BlockSpec(memory_space=pltpu.VMEM)
+    return pl.pallas_call(
+        ready_body,
+        out_shape=(
+            jax.ShapeDtypeStruct((EARLY, TILE, TILE), BF16),
+            jax.ShapeDtypeStruct((BLK, x.shape[0] * TILE), BF16),
+        ),
+        in_specs=[vmem] * 2,
+        out_specs=(vmem, vmem),
+        name="ready",
+        compiler_params=params(),
+        cost_estimate=cost(2 * 10**9, 2 * EARLY * TILE * TILE),
+    )(taps, x)
+
+
+def multiply(s_ref, weights, blocks, shifts, o_ref, part, rows, acc, held, sem):
     x = s_ref[0]
     core = s_ref[1]
-    chans, depth = own_ref.shape
+    chans, depth = weights[0].shape
     size = rows.shape[0] // 4
-    moves = [(own_ref, weight, 0), (other_ref, weight, chans)]
     for ref, (shift, at) in zip(blocks, shifts):
         spot = lax.rem(x + shift, 4) * size + at
-        moves.append((ref, rows, pl.multiple_of(spot, 32)))
-    copies = []
-    for k in range(depth // STEP):
-        span = pl.ds(k * STEP, STEP)
-        for i, (ref, held, spot) in enumerate(moves):
-            copy = pltpu.make_async_copy(
-                ref.at[:, span], held.at[pl.ds(spot, ref.shape[0]), span], sem.at[k, i]
-            )
-            copy.start()
-            copies.append(copy)
-    width = rows.shape[0]
-    if join:
-        o_ref[:, :width] = refs[count][...]
+        rows[pl.ds(pl.multiple_of(spot, 32), ref.shape[0]), :] = ref[...]
     dims = (((1,), (1,)), ((), ()))
     for k in range(depth // STEP):
-        for copy in copies[k * len(moves) : (k + 1) * len(moves)]:
-            copy.wait()
         at = slice(k * STEP, (k + 1) * STEP)
-        for half in range(2):
+        for half, ref in enumerate(weights):
             spot = slice(half * chans, (half + 1) * chans)
-            value = mm(weight[spot, at], rows[:, at], dims)
+            value = mm(ref[:, at], rows[:, at], dims)
             if k:
                 acc[spot, :] += value
             else:
                 acc[spot, :] = value
-    to = slice(join * width, (join + 1) * width)
-    at = pl.multiple_of(core * chans, chans)
-    o_ref[pl.ds(at, chans), to] = acc[:chans, :].astype(BF16)
-    at = pl.multiple_of((1 - core) * chans, chans)
-    o_ref[pl.ds(at, chans), to] = acc[chans:, :].astype(BF16)
-
-
-def project(spots, own, other, blocks, shifts, first=None):
+    copies = []
+    for half in range(2):
+        held[half] = acc[half * chans : (half + 1) * chans, :].astype(BF16)
+        to = core if half == 0 else 1 - core
+        at = pl.ds(pl.multiple_of(to * chans, chans), chans)
+        lanes = pl.ds(part * rows.shape[0], rows.shape[0])
+        copies.append(
+            pltpu.make_async_copy(held.at[half], o_ref.at[at, lanes], sem.at[half])
+        )
+        copies[-1].start()
+    for copy in copies:
+        copy.wait()
+
+
+def first_body(s_ref, *refs, shifts):
+    count = len(shifts)
+    weights, blocks, later = refs[:2], refs[2 : 2 + count], refs[2 + count]
+    o_ref, keep_ref, rows, acc, held, sem = refs[3 + count :]
+    keep = pltpu.make_async_copy(later, keep_ref, sem.at[2])
+    keep.start()
+    multiply(s_ref, weights, blocks, shifts, o_ref, 0, rows, acc, held, sem)
+    keep.wait()
+
+
+def second_body(s_ref, *refs, shifts):
+    count = len(shifts)
+    weights, blocks = refs[:2], refs[2 : 2 + count]
+    o_ref, rows, acc, held, sem = refs[3 + count :]
+    multiply(s_ref, weights, blocks, shifts, o_ref, 1, rows, acc, held, sem)
+
+
+def project(spots, own, other, blocks, shifts, later=None, g=None):
     chans, depth = own.shape
     rows = sum(b.shape[0] for b in blocks)
-    extra = [] if first is None else [first]
-    join = len(extra)
+    whole = jax.ShapeDtypeStruct((2 * chans, 2 * rows), BF16)
+    anywhere = pl.BlockSpec(memory_space=pl.ANY)
+    vmem = pl.BlockSpec(memory_space=pltpu.VMEM)
+    if g is None:
+        body, extra, out = first_body, later, (whole, jax.ShapeDtypeStruct(later.shape, BF16))
+        out_specs, aliases = (anywhere, vmem), {}
+    else:
+        body, extra, out = second_body, g, whole
+        out_specs, aliases = anywhere, {3 + len(blocks): 0}
     return pl.pallas_call(
-        functools.partial(project_body, shifts=shifts, join=join),
-        out_shape=jax.ShapeDtypeStruct((2 * chans, (1 + join) * rows), BF16),
+        functools.partial(body, shifts=shifts),
+        out_shape=out,
         in_specs=[pl.BlockSpec(memory_space=pltpu.SMEM)]
-        + [pl.BlockSpec(memory_space=pl.ANY)] * (2 + len(blocks))
-        + [pl.BlockSpec(memory_space=pltpu.VMEM)] * join,
+        + [vmem] * (2 + len(blocks))
+        + [anywhere],
+        out_specs=out_specs,
+        input_output_aliases=aliases,
         scratch_shapes=[
-            pltpu.VMEM((2 * chans, depth), BF16),
             pltpu.VMEM((rows, depth), BF16),
             pltpu.VMEM((2 * chans, rows), F32),
-            pltpu.SemaphoreType.DMA((depth // STEP, 2 + len(blocks))),
+            pltpu.VMEM((2, chans, rows), BF16),
+            pltpu.SemaphoreType.DMA((3,)),
         ],
         name="project",
         compiler_params=params(),
         cost_estimate=cost(4 * chans * rows * depth, 2 * depth * (2 * chans + rows)),
-    )(spots, own, other, *blocks, *extra)
-
-
-def conv_body(s_ref, g_ref, x_ref, f_ref, o_ref, gb, acc, corr, t_ref):
-    zhi = s_ref[0]
+    )(spots, own, other, *blocks, extra)
+
+
+def conv_body(s_ref, g_ref, x_ref, t_ref, f_ref, o_ref, gb, acc, corr, late):
+    zhi = s_ref[2]
     width = g_ref.shape[1]
     senders = g_ref.shape[0] // 2
     nb = 4 * senders
@@ -164,26 +218,20 @@
             else:
                 corr[part, at, :] += piece
 
-    flip = (iota((TILE, TILE), 0) + iota((TILE, TILE), 1) == TILE - 1).astype(BF16)
-    turned = mm(f_ref[...], flip)
-    t_ref[0] = jnp.zeros((TILE, TILE), BF16)
-
-    def make_tile(k):
-        before = turned[k - 1 : k] if k else jnp.zeros((1, TILE), F32)
-        line = jnp.concatenate([before, turned[k : k + 1]], axis=1)
-        spread = jnp.broadcast_to(line, (TILE, 2 * TILE))
-        turn = pltpu.roll(spread, 1, 1, stride=1, stride_axis=0)
-        t_ref[k + 1] = turn[:, :TILE].astype(BF16)
-
-    full_x = jnp.concatenate([x_ref[s] for s in range(senders)], axis=1)
+    turned = turn_taps(f_ref)
+
+    def tile_at(index):
+        return t_ref[index] if index < EARLY else late[index - EARLY]
+
     for d in range(nb):
-        make_tile(2 * d)
-        make_tile(2 * d + 1)
+        for k in (2 * d, 2 * d + 1):
+            if k + 1 >= EARLY:
+                late[k + 1 - EARLY] = toeplitz_tile(turned, k)
         span = -(-(nb - d) * width // BLK) * BLK
         moved = gb[d * width : d * width + span, :]
-        mid = t_ref[2 * d + 1]
-        up = t_ref[2 * d + 2]
-        down = t_ref[2 * d]
+        mid = tile_at(2 * d + 1)
+        up = tile_at(2 * d + 2)
+        down = tile_at(2 * d)
         tile = jnp.concatenate(
             [
                 jnp.concatenate([mid, down], axis=1),
@@ -195,7 +243,7 @@
             acc[...] = mm(moved, tile)
         else:
             acc[:span, :] += mm(moved, tile)
-        prod = mm(full_x[:, :span], moved)
+        prod = mm(x_ref[:, :span], moved)
         put(2 * d, prod[:TILE, :TILE], fresh=d == 0)
         put(2 * d + 1, prod[:TILE, TILE:] + prod[TILE:, :TILE], fresh=True)
         put(2 * d + 2, prod[TILE:, TILE:], fresh=True)
@@ -241,7 +289,7 @@
         o_ref[s, at + 2 * TAIL :, :] = third
 
 
-def convolve(spot, g, xt, taps):
+def convolve(spot, g, xt, tiles, taps):
     senders = g.shape[0] // 2
     width = g.shape[1]
     nb = 4 * senders
@@ -250,17 +298,17 @@
         conv_body,
         out_shape=jax.ShapeDtypeStruct((senders, 8 * width + 3 * TAIL, TILE), BF16),
         in_specs=[pl.BlockSpec(memory_space=pltpu.SMEM)]
-        + [pl.BlockSpec(memory_space=pltpu.VMEM)] * 3,
+        + [pl.BlockSpec(memory_space=pltpu.VMEM)] * 4,
         scratch_shapes=[
             pltpu.VMEM((top + BLK, BLK), BF16),
             pltpu.VMEM((top, BLK), F32),
             pltpu.VMEM((TILE // PART, (2 * nb + 1) * PART, TILE), F32),
-            pltpu.VMEM((2 * nb + 1, TILE, TILE), BF16),
+            pltpu.VMEM((2 * nb + 1 - EARLY, TILE, TILE), BF16),
         ],
         name="convolve",
         compiler_params=params(),
         cost_estimate=cost(6 * 10**9, 4 * 10**6),
-    )(spot, g, xt, taps)
+    )(spot, g, xt, tiles, taps)
 
 
 def finish_body(m_ref, o_ref, f_ref):
@@ -304,6 +352,8 @@
     core = lax.axis_index("core").astype(jnp.int32)
     zhi = lax.axis_index("zhi").astype(jnp.int32)
     half = grad_out.shape[0] // 2
+    spots = jnp.stack([x, core, zhi])
+    spots, grad_out = lax.optimization_barrier((spots, grad_out))
     before = lax.ppermute(grad_out, "x", X_UP)
     after = lax.ppermute(grad_out, "x", X_DOWN)
     near_own = lax.ppermute(grad_out, near, Z_NEAR)
@@ -318,19 +368,19 @@
     near_far_b = lax.ppermute(far_b, near, Z_NEAR)
     taps = lax.dynamic_index_in_dim(filters, lax.axis_index(seq), 0, False)
     taps = taps.reshape(-1, TILE)
-    spots = jnp.stack([x, core])
+    tiles, xt = ready(taps, turned)
     shifts = [(0, 0), (3, 0), (1, 0), (2, 0), (2, half)]
-    g = project(
+    g, near_own = project(
         spots, out_weight, other_weight,
-        [grad_out, before, after, far_a, far_b], shifts,
+        [grad_out, before, after, far_a, far_b], shifts, later=near_own,
     )
     g = project(
         spots, out_weight, other_weight,
-        [near_own, near_before, near_after, near_far_a, near_far_b], shifts, g,
+        [near_own, near_before, near_after, near_far_a, near_far_b], shifts, g=g,
     )
     g = g.reshape(2 * groups, width, -1)
     g = lax.all_to_all(g, ("core",) + seq, 0, 0, tiled=True)
-    major = convolve(zhi.reshape(1), g, turned, taps)
+    major = convolve(spots, g, xt, tiles, taps)
     major = lax.all_to_all(major, seq, 0, 0, tiled=True)
     return finish(major)
 

time: 88.8 us -> 88.3 us (level)
  waiting for transfers between devices: 25 us -> 22.4 us
  Pallas kernels: 17.4 us -> 18.8 us
    all_to_all x1, waiting for transfers between devices: 11 us -> 8.69 us  [on_device(): g = lax.all_to_all(g, ('core',) + seq, 0, 0, tiled=True)]
    pallas_call x2 -> x3, Pallas kernels: 7.86 us -> 9.88 us  [the longest x2 7.58 us: project(): pl.pallas_call(functools.partial(body, shifts=shifts), out_shape=out, in_...]
  transfers between devices with their start and end apart: 12 -> 12, of which waited for: 4 -> 4; matrix products, arithmetic and copies ran while one was open for 1% -> 2% of each run, Pallas kernels for 10% -> 13%
where the time goes in v3:
time: 88.3 us; the launch traced here: 87.8 us
  starting transfers between devices  28.5 us (32%)
  waiting for transfers between devices  22.4 us (25%)
  Pallas kernels  18.8 us (21%)
  blocking collectives  12.8 us (14%)
  local copies, waits for them, and re-layouts  4.44 us (5%)
    all_to_all x1, blocking collectives, on_device(): major = lax.all_to_all(major, seq, 0, 0, tiled=True)  12.8 us
    all_to_all x1, waiting for transfers between devices, on_device(): g = lax.all_to_all(g, ('core',) + seq, 0, 0, tiled=True)  8.69 us
    ppermute x1, waiting for transfers between devices, on_device(): before = lax.ppermute(grad_out, 'x', X_UP)  8.35 us
    pallas_call x2, Pallas kernels, project(): pl.pallas_call(functools.partial(body, shifts=shifts), out_shape=out, in_...  7.58 us
    pallas_call x1, Pallas kernels, convolve(): pl.pallas_call(conv_body, out_shape=jax.ShapeDtypeStruct((senders, 8 * wi...  6.53 us
    all_to_all x1, starting transfers between devices, on_device(): turned = lax.all_to_all(turned, seq, 0, 0, tiled=True)  5.94 us
    all_to_all x1, starting transfers between devices, on_device(): g = lax.all_to_all(g, ('core',) + seq, 0, 0, tiled=True)  4.37 us
    ppermute x1, starting transfers between devices, on_device(): near_own = lax.ppermute(grad_out, near, Z_NEAR)  4.15 us
  transfers between devices with their start and end apart: 12, of which 4 were waited for; matrix products, arithmetic and copies ran while one was open for 2% of the time, Pallas kernels for 13%

profile of v3, /device:TPU:0, one launch (start us, length us, event | category | flops | bytes accessed | tf_op | source)
XLA Modules:
  0.0 87.8 jit_solution(11487628682017758590)
XLA Ops:
  0.8 1.6 %collective-permute-start.1 = (bf16[64,4096]{1,0:T(8,128)(2,1)}, bf16[64,4096]{1,0:T(8,128)(2,1)S(1)}, u32[]{:S(2)}, u32[]{:S(2)}) collective-permute-start(bf16[64,4096]{1,0:T(8,128)(2,1)} %refs_2_), channel_id=1, source_target_pairs={{0,2},{2,4},{4,6},{6,0},{1,3},{3,5},{5,7},{7,1},{8,10},{10,12},{12... | collective-permute-start | bytes 1572872 | tf_op jit(solution)/shard_map/ppermute | solution.py:357
  2.4 1.6 %collective-permute-start.2 = (bf16[64,4096]{1,0:T(8,128)(2,1)}, bf16[64,4096]{1,0:T(8,128)(2,1)S(1)}, u32[]{:S(2)}, u32[]{:S(2)}) collective-permute-start(bf16[64,4096]{1,0:T(8,128)(2,1)} %refs_2_), channel_id=1, source_target_pairs={{0,6},{2,0},{4,2},{6,4},{1,7},{3,1},{5,3},{7,5},{8,14},{10,8},{12,... | collective-permute-start | bytes 1572872 | tf_op jit(solution)/shard_map/ppermute | solution.py:358
  4.1 4.1 %collective-permute-start.5 = (bf16[64,4096]{1,0:T(8,128)(2,1)}, bf16[64,4096]{1,0:T(8,128)(2,1)}, u32[]{:S(2)}, u32[]{:S(2)}) collective-permute-start(bf16[64,4096]{1,0:T(8,128)(2,1)} %refs_2_), channel_id=1, source_target_pairs={{0,24},{8,16},{16,8},{24,0},{1,25},{9,17},{17,9},{25,1},{2,26},{10... | collective-permute-start | bytes 1572872 | tf_op jit(solution)/shard_map/ppermute | solution.py:359
  8.2 8.3 %collective-permute-done.1.refs_3_ = bf16[64,4096]{1,0:T(8,128)(2,1)S(1)} collective-permute-done((bf16[64,4096]{1,0:T(8,128)(2,1)}, bf16[64,4096]{1,0:T(8,128)(2,1)S(1)}, u32[]{:S(2)}, u32[]{:S(2)}) %collective-permute-start.1) | collective-permute-done | bytes 524320 | tf_op jit(solution)/shard_map/ppermute | solution.py:357
  16.6 0.7 slice.8
  17.7 0.7 slice.9
  18.4 2.8 %collective-permute-start.4 = (bf16[32,4096]{1,0:T(8,128)(2,1)}, bf16[32,4096]{1,0:T(8,128)(2,1)}, u32[]{:S(2)}, u32[]{:S(2)}) collective-permute-start(bf16[32,4096]{1,0:T(8,128)(2,1)} %slice.9), channel_id=1, source_target_pairs={{0,6},{2,0},{4,2},{6,4},{1,7},{3,1},{5,3},{7,5},{8,14},{10,8},{12,... | collective-permute-start | bytes 786440 | tf_op jit(solution)/shard_map/ppermute | solution.py:362
  21.3 3.2 %collective-permute-start.7 = (bf16[64,4096]{1,0:T(8,128)(2,1)}, bf16[64,4096]{1,0:T(8,128)(2,1)}, u32[]{:S(2)}, u32[]{:S(2)}) collective-permute-start(bf16[64,4096]{1,0:T(8,128)(2,1)} %collective-permute-done.5.refs_7_), channel_id=1, source_target_pairs={{0,6},{2,0},{4,2},{6,4},{1,7},{3,1},{5,3},{7,5},{8,14},{10,8},{12,... | collective-permute-start | bytes 1572872 | tf_op jit(solution)/shard_map/ppermute | solution.py:366
  24.5 1.0 %copy-done.4 = bf16[1024,256]{1,0:T(8,128)(2,1)S(1)} copy-done((bf16[1024,256]{1,0:T(8,128)(2,1)S(1)}, bf16[1024,256]{1,0:T(8,128)(2,1)}, u32[]{:S(2)}) %copy-start.4) | copy-done | bytes 524312
  25.5 1.4 %prep_input.1 = bf16[8,256,128]{2,1,0:T(8,128)(2,1)S(1)} custom-call(bf16[1024,256]{1,0:T(8,128)(2,1)S(1)} %copy-done.4), custom_call_target="tpu_custom_call" | custom-call | flops 2000000000 | bytes 1048576 | tf_op jit(solution)/shard_map/prep_input/pallas_call | solution.py:61
  26.9 0.8 copy-done.2
  27.7 5.9 %all-to-all-start.1 = ((bf16[8,256,128]{2,1,0:T(8,128)(2,1)}), bf16[8,256,128]{2,1,0:T(8,128)(2,1)}, u32[]{:S(2)}, u32[]{:S(2)}) async-start(bf16[8,256,128]{2,1,0:T(8,128)(2,1)} %copy-done.2), calls=%async_computation.1 | async-start | bytes 1048576 | tf_op jit(solution)/shard_map/all_to_all | solution.py:364
  33.7 4.1 %collective-permute-start.8 = (bf16[32,4096]{1,0:T(8,128)(2,1)S(1)}, bf16[32,4096]{1,0:T(8,128)(2,1)S(1)}, u32[]{:S(2)}, u32[]{:S(2)}) collective-permute-start(bf16[32,4096]{1,0:T(8,128)(2,1)S(1)} %collective-permute-done.3.refs_5_), channel_id=1, source_target_pairs={{0,24},{8,16},{16,8},{24,0},{1,25},{9,17},{17,9},{25,1},{2,26},{10... | collective-permute-start | bytes 786440 | tf_op jit(solution)/shard_map/ppermute | solution.py:367
  37.9 1.0 %copy-done.3 = bf16[64,4096]{1,0:T(8,128)(2,1)S(1)} copy-done((bf16[64,4096]{1,0:T(8,128)(2,1)S(1)}, bf16[64,4096]{1,0:T(8,128)(2,1)}, u32[]{:S(2)}) %copy-start.3) | copy-done | bytes 524312
  39.0 3.7 %project.2 = (bf16[512,512]{1,0:T(8,128)(2,1)}, bf16[64,4096]{1,0:T(8,128)(2,1)S(1)}) custom-call(s32[3]{0:T(128)S(1)} %pad_add_fusion.s_ref, bf16[256,4096]{1,0:T(8,128)(2,1)S(1)} %copy-done.1, bf16[256,4096]{1,0:T(8,128)(2,1)} %collective-permute-done.refs_1_, bf16[64,4096]{1,0:T(8,128)(2,1)S(1)} %copy-done.3, ...), custom_call_target="tpu_custom_call" | custom-call | flops 1073741824 | bytes 6291456 | tf_op jit(solution)/shard_map/project/pallas_call | solution.py:169
  42.7 2.3 %collective-permute-done.8.refs_5_ = bf16[32,4096]{1,0:T(8,128)(2,1)S(1)} collective-permute-done((bf16[32,4096]{1,0:T(8,128)(2,1)S(1)}, bf16[32,4096]{1,0:T(8,128)(2,1)S(1)}, u32[]{:S(2)}, u32[]{:S(2)}) %collective-permute-start.8) | collective-permute-done | bytes 262176 | tf_op jit(solution)/shard_map/ppermute | solution.py:367
  45.0 3.0 %collective-permute-done.9.refs_6_ = bf16[32,4096]{1,0:T(8,128)(2,1)S(1)} collective-permute-done((bf16[32,4096]{1,0:T(8,128)(2,1)}, bf16[32,4096]{1,0:T(8,128)(2,1)S(1)}, u32[]{:S(2)}, u32[]{:S(2)}) %collective-permute-start.9) | collective-permute-done | bytes 262176 | tf_op jit(solution)/shard_map/ppermute | solution.py:368
  48.0 3.9 %project.3 = bf16[512,512]{1,0:T(8,128)(2,1)} custom-call(s32[3]{0:T(128)S(1)} %pad_add_fusion.s_ref, bf16[256,4096]{1,0:T(8,128)(2,1)S(1)} %copy-done.1, bf16[256,4096]{1,0:T(8,128)(2,1)} %collective-permute-done.refs_1_, bf16[64,4096]{1,0:T(8,128)(2,1)S(1)} %get-tuple-element.10.refs_2_, ...), custom_call_target="tpu_custom_call", output_to_operand_aliasing={{}: (8, {})} | custom-call | flops 1073741824 | bytes 6291456 | tf_op jit(solution)/shard_map/project/pallas_call | solution.py:169
  51.9 4.4 %all-to-all-start = ((bf16[16,32,512]{2,1,0:T(8,128)(2,1)}), bf16[16,32,512]{2,1,0:T(8,128)(2,1)S(1)}, u32[]{:S(2)}, u32[]{:S(2)}) async-start(bf16[16,32,512]{2,1,0:T(8,128)(2,1)} %bitcast.3), calls=%async_computation | async-start | bytes 1048576 | tf_op jit(solution)/shard_map/all_to_all | solution.py:382
  56.4 2.3 %ready.1 = (bf16[56,128,128]{2,1,0:T(8,128)(2,1)S(1)}, bf16[256,1024]{1,0:T(8,128)(2,1)S(1)}) custom-call(bf16[64,128]{1,0:T(8,128)(2,1)S(1)} %bitcast.5, bf16[8,256,128]{2,1,0:T(8,128)(2,1)} %all-to-all-done.1.x_ref), custom_call_target="tpu_custom_call" | custom-call | flops 2000000000 | bytes 1835008 | tf_op jit(solution)/shard_map/ready/pallas_call | solution.py:94
  58.7 8.7 %all-to-all-done.g_ref = bf16[16,32,512]{2,1,0:T(8,128)(2,1)S(1)} async-done(((bf16[16,32,512]{2,1,0:T(8,128)(2,1)}), bf16[16,32,512]{2,1,0:T(8,128)(2,1)S(1)}, u32[]{:S(2)}, u32[]{:S(2)}) %all-to-all-start) | async-done | bytes 524320 | tf_op jit(solution)/shard_map/all_to_all | solution.py:382
  67.4 6.5 %convolve.1 = bf16[8,280,128]{2,1,0:T(8,128)(2,1)S(1)} custom-call(s32[3]{0:T(128)S(1)} %pad_add_fusion.s_ref, bf16[16,32,512]{2,1,0:T(8,128)(2,1)S(1)} %all-to-all-done.g_ref, bf16[256,1024]{1,0:T(8,128)(2,1)S(1)} %get-tuple-element.12.x_ref, bf16[56,128,128]{2,1,0:T(8,128)(2,1)S(1)} %get-tuple-element.13.t_ref, bf16[64,128]{1,0:T(8,128)(2,1)S(1)} %bitcast.6), custom_call_target="tpu_custom_call" | custom-call | flops 6000000000 | bytes 4000000 | tf_op jit(solution)/shard_map/convolve/pallas_call | solution.py:297
  73.9 12.8 %all_to_all.15.m_ref = bf16[8,280,128]{2,1,0:T(8,128)(2,1)S(1)} all-to-all(bf16[8,280,128]{2,1,0:T(8,128)(2,1)S(1)} %convolve.1), channel_id=1, replica_groups=mesh['y'=4,'zlo'=2,'zhi'=2,'x'=4,'core'=2] {'y','zlo'}, dimensions={0} | all-to-all | bytes 1146880 | tf_op jit(solution)/shard_map/all_to_all | solution.py:384
  86.8 1.0 %finish.1 = (bf16[1024,256]{1,0:T(8,128)(2,1)}, f32[8,1024]{1,0:T(8,128)}) custom-call(bf16[8,280,128]{2,1,0:T(8,128)(2,1)S(1)} %all_to_all.15.m_ref), custom_call_target="tpu_custom_call" | custom-call | flops 1000000 | bytes 1146880 | tf_op jit(solution)/shard_map/finish/pallas_call | solution.py:334
  (21 shorter events, 0.8 us)
Async XLA Ops:
  0.6 55.6 %copy-start = (bf16[8,8192]{1,0:T(8,128)(2,1)S(1)}, bf16[8,8192]{1,0:T(8,128)(2,1)}, u32[]{:S(2)}) copy-start(bf16[8,8192]{1,0:T(8,128)(2,1)} %param.7) | copy-start | bytes 393220
  0.6 37.3 %collective-permute-start = (bf16[256,4096]{1,0:T(8,128)(2,1)}, bf16[256,4096]{1,0:T(8,128)(2,1)}, u32[]{:S(2)}, u32[]{:S(2)}) collective-permute-start(bf16[256,4096]{1,0:T(8,128)(2,1)} %refs_0_.3), channel_id=1, source_target_pairs={{0,1},{1,0},{2,3},{3,2},{4,5},{5,4},{6,7},{7,6},{8,9},{9,8},{10,11... | collective-permute-start | bytes 6291464 | tf_op jit(solution)/shard_map/ppermute | solution.py:360
  0.8 15.7 %collective-permute-start.1 = (bf16[64,4096]{1,0:T(8,128)(2,1)}, bf16[64,4096]{1,0:T(8,128)(2,1)S(1)}, u32[]{:S(2)}, u32[]{:S(2)}) collective-permute-start(bf16[64,4096]{1,0:T(8,128)(2,1)} %refs_2_), channel_id=1, source_target_pairs={{0,2},{2,4},{4,6},{6,0},{1,3},{3,5},{5,7},{7,1},{8,10},{10,12},{12... | collective-permute-start | bytes 1572872 | tf_op jit(solution)/shard_map/ppermute | solution.py:357
  2.4 15.2 %collective-permute-start.2 = (bf16[64,4096]{1,0:T(8,128)(2,1)}, bf16[64,4096]{1,0:T(8,128)(2,1)S(1)}, u32[]{:S(2)}, u32[]{:S(2)}) collective-permute-start(bf16[64,4096]{1,0:T(8,128)(2,1)} %refs_2_), channel_id=1, source_target_pairs={{0,6},{2,0},{4,2},{6,4},{1,7},{3,1},{5,3},{7,5},{8,14},{10,8},{12,... | collective-permute-start | bytes 1572872 | tf_op jit(solution)/shard_map/ppermute | solution.py:358
  4.1 17.2 %collective-permute-start.5 = (bf16[64,4096]{1,0:T(8,128)(2,1)}, bf16[64,4096]{1,0:T(8,128)(2,1)}, u32[]{:S(2)}, u32[]{:S(2)}) collective-permute-start(bf16[64,4096]{1,0:T(8,128)(2,1)} %refs_2_), channel_id=1, source_target_pairs={{0,24},{8,16},{16,8},{24,0},{1,25},{9,17},{17,9},{25,1},{2,26},{10... | collective-permute-start | bytes 1572872 | tf_op jit(solution)/shard_map/ppermute | solution.py:359
  17.3 16.4 %collective-permute-start.3 = (bf16[32,4096]{1,0:T(8,128)(2,1)}, bf16[32,4096]{1,0:T(8,128)(2,1)S(1)}, u32[]{:S(2)}, u32[]{:S(2)}) collective-permute-start(bf16[32,4096]{1,0:T(8,128)(2,1)} %slice.8), channel_id=1, source_target_pairs={{0,2},{2,4},{4,6},{6,0},{1,3},{3,5},{5,7},{7,1},{8,10},{10,12},{12... | collective-permute-start | bytes 786440 | tf_op jit(solution)/shard_map/ppermute | solution.py:361
  18.4 19.4 %collective-permute-start.4 = (bf16[32,4096]{1,0:T(8,128)(2,1)}, bf16[32,4096]{1,0:T(8,128)(2,1)}, u32[]{:S(2)}, u32[]{:S(2)}) collective-permute-start(bf16[32,4096]{1,0:T(8,128)(2,1)} %slice.9), channel_id=1, source_target_pairs={{0,6},{2,0},{4,2},{6,4},{1,7},{3,1},{5,3},{7,5},{8,14},{10,8},{12,... | collective-permute-start | bytes 786440 | tf_op jit(solution)/shard_map/ppermute | solution.py:362
  21.3 26.7 %collective-permute-start.6 = (bf16[64,4096]{1,0:T(8,128)(2,1)}, bf16[64,4096]{1,0:T(8,128)(2,1)}, u32[]{:S(2)}, u32[]{:S(2)}) collective-permute-start(bf16[64,4096]{1,0:T(8,128)(2,1)} %collective-permute-done.5.refs_7_), channel_id=1, source_target_pairs={{0,2},{2,4},{4,6},{6,0},{1,3},{3,5},{5,7},{7,1},{8,10},{10,12},{12... | collective-permute-start | bytes 1572872 | tf_op jit(solution)/shard_map/ppermute | solution.py:365
  21.3 26.7 %collective-permute-start.7 = (bf16[64,4096]{1,0:T(8,128)(2,1)}, bf16[64,4096]{1,0:T(8,128)(2,1)}, u32[]{:S(2)}, u32[]{:S(2)}) collective-permute-start(bf16[64,4096]{1,0:T(8,128)(2,1)} %collective-permute-done.5.refs_7_), channel_id=1, source_target_pairs={{0,6},{2,0},{4,2},{6,4},{1,7},{3,1},{5,3},{7,5},{8,14},{10,8},{12,... | collective-permute-start | bytes 1572872 | tf_op jit(solution)/shard_map/ppermute | solution.py:366
  24.5 1.0 %copy-start.4 = (bf16[1024,256]{1,0:T(8,128)(2,1)S(1)}, bf16[1024,256]{1,0:T(8,128)(2,1)}, u32[]{:S(2)}) copy-start(bf16[1024,256]{1,0:T(8,128)(2,1)} %x_ref.1) | copy-start | bytes 1572868
  25.5 12.4 %copy-start.1 = (bf16[256,4096]{1,0:T(8,128)(2,1)S(1)}, bf16[256,4096]{1,0:T(8,128)(2,1)}, u32[]{:S(2)}) copy-start(bf16[256,4096]{1,0:T(8,128)(2,1)} %refs_0_.3) | copy-start | bytes 6291460
  26.9 0.8 copy-start.2
  27.7 24.1 %all-to-all-start.1 = ((bf16[8,256,128]{2,1,0:T(8,128)(2,1)}), bf16[8,256,128]{2,1,0:T(8,128)(2,1)}, u32[]{:S(2)}, u32[]{:S(2)}) async-start(bf16[8,256,128]{2,1,0:T(8,128)(2,1)} %copy-done.2), calls=%async_computation.1 | async-start | bytes 1048576 | tf_op jit(solution)/shard_map/all_to_all | solution.py:364
  33.7 11.3 %collective-permute-start.8 = (bf16[32,4096]{1,0:T(8,128)(2,1)S(1)}, bf16[32,4096]{1,0:T(8,128)(2,1)S(1)}, u32[]{:S(2)}, u32[]{:S(2)}) collective-permute-start(bf16[32,4096]{1,0:T(8,128)(2,1)S(1)} %collective-permute-done.3.refs_5_), channel_id=1, source_target_pairs={{0,24},{8,16},{16,8},{24,0},{1,25},{9,17},{17,9},{25,1},{2,26},{10... | collective-permute-start | bytes 786440 | tf_op jit(solution)/shard_map/ppermute | solution.py:367
  37.8 10.1 %collective-permute-start.9 = (bf16[32,4096]{1,0:T(8,128)(2,1)}, bf16[32,4096]{1,0:T(8,128)(2,1)S(1)}, u32[]{:S(2)}, u32[]{:S(2)}) collective-permute-start(bf16[32,4096]{1,0:T(8,128)(2,1)} %collective-permute-done.4.refs_6_), channel_id=1, source_target_pairs={{0,24},{8,16},{16,8},{24,0},{1,25},{9,17},{17,9},{25,1},{2,26},{10... | collective-permute-start | bytes 786440 | tf_op jit(solution)/shard_map/ppermute | solution.py:368
  37.9 1.0 %copy-start.3 = (bf16[64,4096]{1,0:T(8,128)(2,1)S(1)}, bf16[64,4096]{1,0:T(8,128)(2,1)}, u32[]{:S(2)}) copy-start(bf16[64,4096]{1,0:T(8,128)(2,1)} %refs_2_) | copy-start | bytes 1572868
  51.9 15.5 %all-to-all-start = ((bf16[16,32,512]{2,1,0:T(8,128)(2,1)}), bf16[16,32,512]{2,1,0:T(8,128)(2,1)S(1)}, u32[]{:S(2)}, u32[]{:S(2)}) async-start(bf16[16,32,512]{2,1,0:T(8,128)(2,1)} %bitcast.3), calls=%async_computation | async-start | bytes 1048576 | tf_op jit(solution)/shard_map/all_to_all | solution.py:382

commit v4 on v3

--- a/solution.py
+++ b/solution.py
@@ -17,6 +17,7 @@
 TAIL = 8
 STEP = 1024
 EARLY = 56
+BATCH = 2
 VMEM_MIB = 24
 X_UP = [(i, (i + 1) % 4) for i in range(4)]
 X_DOWN = [(i, (i - 1) % 4) for i in range(4)]
@@ -223,27 +224,35 @@
     def tile_at(index):
         return t_ref[index] if index < EARLY else late[index - EARLY]
 
-    for d in range(nb):
+    def block_tile(d):
         for k in (2 * d, 2 * d + 1):
             if k + 1 >= EARLY:
                 late[k + 1 - EARLY] = toeplitz_tile(turned, k)
-        span = -(-(nb - d) * width // BLK) * BLK
-        moved = gb[d * width : d * width + span, :]
         mid = tile_at(2 * d + 1)
         up = tile_at(2 * d + 2)
         down = tile_at(2 * d)
-        tile = jnp.concatenate(
+        return jnp.concatenate(
             [
                 jnp.concatenate([mid, down], axis=1),
                 jnp.concatenate([up, mid], axis=1),
             ],
             axis=0,
         )
-        if d == 0:
-            acc[...] = mm(moved, tile)
-        else:
-            acc[:span, :] += mm(moved, tile)
-        prod = mm(x_ref[:, :span], moved)
+
+    for d in range(nb):
+        span = -(-(nb - d) * width // BLK) * BLK
+        if d % BATCH == 0:
+            many = range(d, d + BATCH)
+            moved = [gb[e * width : e * width + span, :] for e in many]
+            value = mm(
+                jnp.concatenate(moved, axis=1),
+                jnp.concatenate([block_tile(e) for e in many], axis=0),
+            )
+            if d == 0:
+                acc[...] = value
+            else:
+                acc[:span, :] += value
+        prod = mm(x_ref[:, :span], gb[d * width : d * width + span, :])
         put(2 * d, prod[:TILE, :TILE], fresh=d == 0)
         put(2 * d + 1, prod[:TILE, TILE:] + prod[TILE:, :TILE], fresh=True)
         put(2 * d + 2, prod[TILE:, TILE:], fresh=True)
@@ -300,7 +309,7 @@
         in_specs=[pl.BlockSpec(memory_space=pltpu.SMEM)]
         + [pl.BlockSpec(memory_space=pltpu.VMEM)] * 4,
         scratch_shapes=[
-            pltpu.VMEM((top + BLK, BLK), BF16),
+            pltpu.VMEM((top + 2 * BLK, BLK), BF16),
             pltpu.VMEM((top, BLK), F32),
             pltpu.VMEM((TILE // PART, (2 * nb + 1) * PART, TILE), F32),
             pltpu.VMEM((2 * nb + 1 - EARLY, TILE, TILE), BF16),

time: 88.3 us -> 88.3 us (level)
  no operation moved by 1% of the time
where the time goes in v4:
time: 88.3 us; the launch traced here: 87.8 us
  starting transfers between devices  28.5 us (32%)
  waiting for transfers between devices  22.4 us (25%)
  Pallas kernels  18.8 us (21%)
  blocking collectives  12.8 us (14%)
  local copies, waits for them, and re-layouts  4.44 us (5%)
    all_to_all x1, blocking collectives, on_device(): major = lax.all_to_all(major, seq, 0, 0, tiled=True)  12.8 us
    all_to_all x1, waiting for transfers between devices, on_device(): g = lax.all_to_all(g, ('core',) + seq, 0, 0, tiled=True)  8.69 us
    ppermute x1, waiting for transfers between devices, on_device(): before = lax.ppermute(grad_out, 'x', X_UP)  8.35 us
    pallas_call x2, Pallas kernels, project(): pl.pallas_call(functools.partial(body, shifts=shifts), out_shape=out, in_...  7.58 us
    pallas_call x1, Pallas kernels, convolve(): pl.pallas_call(conv_body, out_shape=jax.ShapeDtypeStruct((senders, 8 * wi...  6.54 us
    all_to_all x1, starting transfers between devices, on_device(): turned = lax.all_to_all(turned, seq, 0, 0, tiled=True)  5.94 us
    all_to_all x1, starting transfers between devices, on_device(): g = lax.all_to_all(g, ('core',) + seq, 0, 0, tiled=True)  4.37 us
    ppermute x1, starting transfers between devices, on_device(): near_own = lax.ppermute(grad_out, near, Z_NEAR)  4.15 us
  transfers between devices with their start and end apart: 12, of which 4 were waited for; matrix products, arithmetic and copies ran while one was open for 2% of the time, Pallas kernels for 13%

profile of v4, /device:TPU:0, one launch (start us, length us, event | category | flops | bytes accessed | tf_op | source)
XLA Modules:
  0.0 87.8 jit_solution(11797098085153694361)
XLA Ops:
  0.8 1.6 %collective-permute-start.1 = (bf16[64,4096]{1,0:T(8,128)(2,1)}, bf16[64,4096]{1,0:T(8,128)(2,1)S(1)}, u32[]{:S(2)}, u32[]{:S(2)}) collective-permute-start(bf16[64,4096]{1,0:T(8,128)(2,1)} %refs_2_), channel_id=1, source_target_pairs={{0,2},{2,4},{4,6},{6,0},{1,3},{3,5},{5,7},{7,1},{8,10},{10,12},{12... | collective-permute-start | bytes 1572872 | tf_op jit(solution)/shard_map/ppermute | solution.py:366
  2.4 1.6 %collective-permute-start.2 = (bf16[64,4096]{1,0:T(8,128)(2,1)}, bf16[64,4096]{1,0:T(8,128)(2,1)S(1)}, u32[]{:S(2)}, u32[]{:S(2)}) collective-permute-start(bf16[64,4096]{1,0:T(8,128)(2,1)} %refs_2_), channel_id=1, source_target_pairs={{0,6},{2,0},{4,2},{6,4},{1,7},{3,1},{5,3},{7,5},{8,14},{10,8},{12,... | collective-permute-start | bytes 1572872 | tf_op jit(solution)/shard_map/ppermute | solution.py:367
  4.1 4.1 %collective-permute-start.5 = (bf16[64,4096]{1,0:T(8,128)(2,1)}, bf16[64,4096]{1,0:T(8,128)(2,1)}, u32[]{:S(2)}, u32[]{:S(2)}) collective-permute-start(bf16[64,4096]{1,0:T(8,128)(2,1)} %refs_2_), channel_id=1, source_target_pairs={{0,24},{8,16},{16,8},{24,0},{1,25},{9,17},{17,9},{25,1},{2,26},{10... | collective-permute-start | bytes 1572872 | tf_op jit(solution)/shard_map/ppermute | solution.py:368
  8.2 8.3 %collective-permute-done.1.refs_3_ = bf16[64,4096]{1,0:T(8,128)(2,1)S(1)} collective-permute-done((bf16[64,4096]{1,0:T(8,128)(2,1)}, bf16[64,4096]{1,0:T(8,128)(2,1)S(1)}, u32[]{:S(2)}, u32[]{:S(2)}) %collective-permute-start.1) | collective-permute-done | bytes 524320 | tf_op jit(solution)/shard_map/ppermute | solution.py:366
  16.6 0.7 slice.8
  17.7 0.7 slice.9
  18.4 2.8 %collective-permute-start.4 = (bf16[32,4096]{1,0:T(8,128)(2,1)}, bf16[32,4096]{1,0:T(8,128)(2,1)}, u32[]{:S(2)}, u32[]{:S(2)}) collective-permute-start(bf16[32,4096]{1,0:T(8,128)(2,1)} %slice.9), channel_id=1, source_target_pairs={{0,6},{2,0},{4,2},{6,4},{1,7},{3,1},{5,3},{7,5},{8,14},{10,8},{12,... | collective-permute-start | bytes 786440 | tf_op jit(solution)/shard_map/ppermute | solution.py:371
  21.3 3.2 %collective-permute-start.7 = (bf16[64,4096]{1,0:T(8,128)(2,1)}, bf16[64,4096]{1,0:T(8,128)(2,1)}, u32[]{:S(2)}, u32[]{:S(2)}) collective-permute-start(bf16[64,4096]{1,0:T(8,128)(2,1)} %collective-permute-done.5.refs_7_), channel_id=1, source_target_pairs={{0,6},{2,0},{4,2},{6,4},{1,7},{3,1},{5,3},{7,5},{8,14},{10,8},{12,... | collective-permute-start | bytes 1572872 | tf_op jit(solution)/shard_map/ppermute | solution.py:375
  24.5 1.0 %copy-done.4 = bf16[1024,256]{1,0:T(8,128)(2,1)S(1)} copy-done((bf16[1024,256]{1,0:T(8,128)(2,1)S(1)}, bf16[1024,256]{1,0:T(8,128)(2,1)}, u32[]{:S(2)}) %copy-start.4) | copy-done | bytes 524312
  25.5 1.4 %prep_input.1 = bf16[8,256,128]{2,1,0:T(8,128)(2,1)S(1)} custom-call(bf16[1024,256]{1,0:T(8,128)(2,1)S(1)} %copy-done.4), custom_call_target="tpu_custom_call" | custom-call | flops 2000000000 | bytes 1048576 | tf_op jit(solution)/shard_map/prep_input/pallas_call | solution.py:62
  26.9 0.8 copy-done.2
  27.7 5.9 %all-to-all-start.1 = ((bf16[8,256,128]{2,1,0:T(8,128)(2,1)}), bf16[8,256,128]{2,1,0:T(8,128)(2,1)}, u32[]{:S(2)}, u32[]{:S(2)}) async-start(bf16[8,256,128]{2,1,0:T(8,128)(2,1)} %copy-done.2), calls=%async_computation.1 | async-start | bytes 1048576 | tf_op jit(solution)/shard_map/all_to_all | solution.py:373
  33.7 4.1 %collective-permute-start.8 = (bf16[32,4096]{1,0:T(8,128)(2,1)S(1)}, bf16[32,4096]{1,0:T(8,128)(2,1)S(1)}, u32[]{:S(2)}, u32[]{:S(2)}) collective-permute-start(bf16[32,4096]{1,0:T(8,128)(2,1)S(1)} %collective-permute-done.3.refs_5_), channel_id=1, source_target_pairs={{0,24},{8,16},{16,8},{24,0},{1,25},{9,17},{17,9},{25,1},{2,26},{10... | collective-permute-start | bytes 786440 | tf_op jit(solution)/shard_map/ppermute | solution.py:376
  37.9 1.0 %copy-done.3 = bf16[64,4096]{1,0:T(8,128)(2,1)S(1)} copy-done((bf16[64,4096]{1,0:T(8,128)(2,1)S(1)}, bf16[64,4096]{1,0:T(8,128)(2,1)}, u32[]{:S(2)}) %copy-start.3) | copy-done | bytes 524312
  39.0 3.7 %project.2 = (bf16[512,512]{1,0:T(8,128)(2,1)}, bf16[64,4096]{1,0:T(8,128)(2,1)S(1)}) custom-call(s32[3]{0:T(128)S(1)} %pad_add_fusion.s_ref, bf16[256,4096]{1,0:T(8,128)(2,1)S(1)} %copy-done.1, bf16[256,4096]{1,0:T(8,128)(2,1)} %collective-permute-done.refs_1_, bf16[64,4096]{1,0:T(8,128)(2,1)S(1)} %copy-done.3, ...), custom_call_target="tpu_custom_call" | custom-call | flops 1073741824 | bytes 6291456 | tf_op jit(solution)/shard_map/project/pallas_call | solution.py:170
  42.7 2.3 %collective-permute-done.8.refs_5_ = bf16[32,4096]{1,0:T(8,128)(2,1)S(1)} collective-permute-done((bf16[32,4096]{1,0:T(8,128)(2,1)S(1)}, bf16[32,4096]{1,0:T(8,128)(2,1)S(1)}, u32[]{:S(2)}, u32[]{:S(2)}) %collective-permute-start.8) | collective-permute-done | bytes 262176 | tf_op jit(solution)/shard_map/ppermute | solution.py:376
  45.0 3.0 %collective-permute-done.9.refs_6_ = bf16[32,4096]{1,0:T(8,128)(2,1)S(1)} collective-permute-done((bf16[32,4096]{1,0:T(8,128)(2,1)}, bf16[32,4096]{1,0:T(8,128)(2,1)S(1)}, u32[]{:S(2)}, u32[]{:S(2)}) %collective-permute-start.9) | collective-permute-done | bytes 262176 | tf_op jit(solution)/shard_map/ppermute | solution.py:377
  48.0 3.9 %project.3 = bf16[512,512]{1,0:T(8,128)(2,1)} custom-call(s32[3]{0:T(128)S(1)} %pad_add_fusion.s_ref, bf16[256,4096]{1,0:T(8,128)(2,1)S(1)} %copy-done.1, bf16[256,4096]{1,0:T(8,128)(2,1)} %collective-permute-done.refs_1_, bf16[64,4096]{1,0:T(8,128)(2,1)S(1)} %get-tuple-element.10.refs_2_, ...), custom_call_target="tpu_custom_call", output_to_operand_aliasing={{}: (8, {})} | custom-call | flops 1073741824 | bytes 6291456 | tf_op jit(solution)/shard_map/project/pallas_call | solution.py:170
  51.9 4.4 %all-to-all-start = ((bf16[16,32,512]{2,1,0:T(8,128)(2,1)}), bf16[16,32,512]{2,1,0:T(8,128)(2,1)S(1)}, u32[]{:S(2)}, u32[]{:S(2)}) async-start(bf16[16,32,512]{2,1,0:T(8,128)(2,1)} %bitcast.3), calls=%async_computation | async-start | bytes 1048576 | tf_op jit(solution)/shard_map/all_to_all | solution.py:391
  56.4 2.3 %ready.1 = (bf16[56,128,128]{2,1,0:T(8,128)(2,1)S(1)}, bf16[256,1024]{1,0:T(8,128)(2,1)S(1)}) custom-call(bf16[64,128]{1,0:T(8,128)(2,1)S(1)} %bitcast.5, bf16[8,256,128]{2,1,0:T(8,128)(2,1)} %all-to-all-done.1.x_ref), custom_call_target="tpu_custom_call" | custom-call | flops 2000000000 | bytes 1835008 | tf_op jit(solution)/shard_map/ready/pallas_call | solution.py:95
  58.7 8.7 %all-to-all-done.g_ref = bf16[16,32,512]{2,1,0:T(8,128)(2,1)S(1)} async-done(((bf16[16,32,512]{2,1,0:T(8,128)(2,1)}), bf16[16,32,512]{2,1,0:T(8,128)(2,1)S(1)}, u32[]{:S(2)}, u32[]{:S(2)}) %all-to-all-start) | async-done | bytes 524320 | tf_op jit(solution)/shard_map/all_to_all | solution.py:391
  67.4 6.5 %convolve.1 = bf16[8,280,128]{2,1,0:T(8,128)(2,1)S(1)} custom-call(s32[3]{0:T(128)S(1)} %pad_add_fusion.s_ref, bf16[16,32,512]{2,1,0:T(8,128)(2,1)S(1)} %all-to-all-done.g_ref, bf16[256,1024]{1,0:T(8,128)(2,1)S(1)} %get-tuple-element.12.x_ref, bf16[56,128,128]{2,1,0:T(8,128)(2,1)S(1)} %get-tuple-element.13.t_ref, bf16[64,128]{1,0:T(8,128)(2,1)S(1)} %bitcast.6), custom_call_target="tpu_custom_call" | custom-call | flops 6000000000 | bytes 4000000 | tf_op jit(solution)/shard_map/convolve/pallas_call | solution.py:306
  73.9 12.8 %all_to_all.15.m_ref = bf16[8,280,128]{2,1,0:T(8,128)(2,1)S(1)} all-to-all(bf16[8,280,128]{2,1,0:T(8,128)(2,1)S(1)} %convolve.1), channel_id=1, replica_groups=mesh['y'=4,'zlo'=2,'zhi'=2,'x'=4,'core'=2] {'y','zlo'}, dimensions={0} | all-to-all | bytes 1146880 | tf_op jit(solution)/shard_map/all_to_all | solution.py:393
  86.8 1.0 %finish.1 = (bf16[1024,256]{1,0:T(8,128)(2,1)}, f32[8,1024]{1,0:T(8,128)}) custom-call(bf16[8,280,128]{2,1,0:T(8,128)(2,1)S(1)} %all_to_all.15.m_ref), custom_call_target="tpu_custom_call" | custom-call | flops 1000000 | bytes 1146880 | tf_op jit(solution)/shard_map/finish/pallas_call | solution.py:343
  (21 shorter events, 0.8 us)
Async XLA Ops:
  0.6 55.6 %copy-start = (bf16[8,8192]{1,0:T(8,128)(2,1)S(1)}, bf16[8,8192]{1,0:T(8,128)(2,1)}, u32[]{:S(2)}) copy-start(bf16[8,8192]{1,0:T(8,128)(2,1)} %param.7) | copy-start | bytes 393220
  0.6 37.3 %collective-permute-start = (bf16[256,4096]{1,0:T(8,128)(2,1)}, bf16[256,4096]{1,0:T(8,128)(2,1)}, u32[]{:S(2)}, u32[]{:S(2)}) collective-permute-start(bf16[256,4096]{1,0:T(8,128)(2,1)} %refs_0_.3), channel_id=1, source_target_pairs={{0,1},{1,0},{2,3},{3,2},{4,5},{5,4},{6,7},{7,6},{8,9},{9,8},{10,11... | collective-permute-start | bytes 6291464 | tf_op jit(solution)/shard_map/ppermute | solution.py:369
  0.8 15.7 %collective-permute-start.1 = (bf16[64,4096]{1,0:T(8,128)(2,1)}, bf16[64,4096]{1,0:T(8,128)(2,1)S(1)}, u32[]{:S(2)}, u32[]{:S(2)}) collective-permute-start(bf16[64,4096]{1,0:T(8,128)(2,1)} %refs_2_), channel_id=1, source_target_pairs={{0,2},{2,4},{4,6},{6,0},{1,3},{3,5},{5,7},{7,1},{8,10},{10,12},{12... | collective-permute-start | bytes 1572872 | tf_op jit(solution)/shard_map/ppermute | solution.py:366
  2.4 15.2 %collective-permute-start.2 = (bf16[64,4096]{1,0:T(8,128)(2,1)}, bf16[64,4096]{1,0:T(8,128)(2,1)S(1)}, u32[]{:S(2)}, u32[]{:S(2)}) collective-permute-start(bf16[64,4096]{1,0:T(8,128)(2,1)} %refs_2_), channel_id=1, source_target_pairs={{0,6},{2,0},{4,2},{6,4},{1,7},{3,1},{5,3},{7,5},{8,14},{10,8},{12,... | collective-permute-start | bytes 1572872 | tf_op jit(solution)/shard_map/ppermute | solution.py:367
  4.1 17.2 %collective-permute-start.5 = (bf16[64,4096]{1,0:T(8,128)(2,1)}, bf16[64,4096]{1,0:T(8,128)(2,1)}, u32[]{:S(2)}, u32[]{:S(2)}) collective-permute-start(bf16[64,4096]{1,0:T(8,128)(2,1)} %refs_2_), channel_id=1, source_target_pairs={{0,24},{8,16},{16,8},{24,0},{1,25},{9,17},{17,9},{25,1},{2,26},{10... | collective-permute-start | bytes 1572872 | tf_op jit(solution)/shard_map/ppermute | solution.py:368
  17.3 16.4 %collective-permute-start.3 = (bf16[32,4096]{1,0:T(8,128)(2,1)}, bf16[32,4096]{1,0:T(8,128)(2,1)S(1)}, u32[]{:S(2)}, u32[]{:S(2)}) collective-permute-start(bf16[32,4096]{1,0:T(8,128)(2,1)} %slice.8), channel_id=1, source_target_pairs={{0,2},{2,4},{4,6},{6,0},{1,3},{3,5},{5,7},{7,1},{8,10},{10,12},{12... | collective-permute-start | bytes 786440 | tf_op jit(solution)/shard_map/ppermute | solution.py:370
  18.4 19.4 %collective-permute-start.4 = (bf16[32,4096]{1,0:T(8,128)(2,1)}, bf16[32,4096]{1,0:T(8,128)(2,1)}, u32[]{:S(2)}, u32[]{:S(2)}) collective-permute-start(bf16[32,4096]{1,0:T(8,128)(2,1)} %slice.9), channel_id=1, source_target_pairs={{0,6},{2,0},{4,2},{6,4},{1,7},{3,1},{5,3},{7,5},{8,14},{10,8},{12,... | collective-permute-start | bytes 786440 | tf_op jit(solution)/shard_map/ppermute | solution.py:371
  21.3 26.7 %collective-permute-start.6 = (bf16[64,4096]{1,0:T(8,128)(2,1)}, bf16[64,4096]{1,0:T(8,128)(2,1)}, u32[]{:S(2)}, u32[]{:S(2)}) collective-permute-start(bf16[64,4096]{1,0:T(8,128)(2,1)} %collective-permute-done.5.refs_7_), channel_id=1, source_target_pairs={{0,2},{2,4},{4,6},{6,0},{1,3},{3,5},{5,7},{7,1},{8,10},{10,12},{12... | collective-permute-start | bytes 1572872 | tf_op jit(solution)/shard_map/ppermute | solution.py:374
  21.3 26.7 %collective-permute-start.7 = (bf16[64,4096]{1,0:T(8,128)(2,1)}, bf16[64,4096]{1,0:T(8,128)(2,1)}, u32[]{:S(2)}, u32[]{:S(2)}) collective-permute-start(bf16[64,4096]{1,0:T(8,128)(2,1)} %collective-permute-done.5.refs_7_), channel_id=1, source_target_pairs={{0,6},{2,0},{4,2},{6,4},{1,7},{3,1},{5,3},{7,5},{8,14},{10,8},{12,... | collective-permute-start | bytes 1572872 | tf_op jit(solution)/shard_map/ppermute | solution.py:375
  24.5 1.0 %copy-start.4 = (bf16[1024,256]{1,0:T(8,128)(2,1)S(1)}, bf16[1024,256]{1,0:T(8,128)(2,1)}, u32[]{:S(2)}) copy-start(bf16[1024,256]{1,0:T(8,128)(2,1)} %x_ref.1) | copy-start | bytes 1572868
  25.5 12.4 %copy-start.1 = (bf16[256,4096]{1,0:T(8,128)(2,1)S(1)}, bf16[256,4096]{1,0:T(8,128)(2,1)}, u32[]{:S(2)}) copy-start(bf16[256,4096]{1,0:T(8,128)(2,1)} %refs_0_.3) | copy-start | bytes 6291460
  26.9 0.8 copy-start.2
  27.7 24.1 %all-to-all-start.1 = ((bf16[8,256,128]{2,1,0:T(8,128)(2,1)}), bf16[8,256,128]{2,1,0:T(8,128)(2,1)}, u32[]{:S(2)}, u32[]{:S(2)}) async-start(bf16[8,256,128]{2,1,0:T(8,128)(2,1)} %copy-done.2), calls=%async_computation.1 | async-start | bytes 1048576 | tf_op jit(solution)/shard_map/all_to_all | solution.py:373
  33.7 11.3 %collective-permute-start.8 = (bf16[32,4096]{1,0:T(8,128)(2,1)S(1)}, bf16[32,4096]{1,0:T(8,128)(2,1)S(1)}, u32[]{:S(2)}, u32[]{:S(2)}) collective-permute-start(bf16[32,4096]{1,0:T(8,128)(2,1)S(1)} %collective-permute-done.3.refs_5_), channel_id=1, source_target_pairs={{0,24},{8,16},{16,8},{24,0},{1,25},{9,17},{17,9},{25,1},{2,26},{10... | collective-permute-start | bytes 786440 | tf_op jit(solution)/shard_map/ppermute | solution.py:376
  37.8 10.1 %collective-permute-start.9 = (bf16[32,4096]{1,0:T(8,128)(2,1)}, bf16[32,4096]{1,0:T(8,128)(2,1)S(1)}, u32[]{:S(2)}, u32[]{:S(2)}) collective-permute-start(bf16[32,4096]{1,0:T(8,128)(2,1)} %collective-permute-done.4.refs_6_), channel_id=1, source_target_pairs={{0,24},{8,16},{16,8},{24,0},{1,25},{9,17},{17,9},{25,1},{2,26},{10... | collective-permute-start | bytes 786440 | tf_op jit(solution)/shard_map/ppermute | solution.py:377
  37.9 1.0 %copy-start.3 = (bf16[64,4096]{1,0:T(8,128)(2,1)S(1)}, bf16[64,4096]{1,0:T(8,128)(2,1)}, u32[]{:S(2)}) copy-start(bf16[64,4096]{1,0:T(8,128)(2,1)} %refs_2_) | copy-start | bytes 1572868
  51.9 15.5 %all-to-all-start = ((bf16[16,32,512]{2,1,0:T(8,128)(2,1)}), bf16[16,32,512]{2,1,0:T(8,128)(2,1)S(1)}, u32[]{:S(2)}, u32[]{:S(2)}) async-start(bf16[16,32,512]{2,1,0:T(8,128)(2,1)} %bitcast.3), calls=%async_computation | async-start | bytes 1048576 | tf_op jit(solution)/shard_map/all_to_all | solution.py:391

commit v5 on v3

--- a/solution.py
+++ b/solution.py
@@ -105,7 +105,7 @@
     )(taps, x)
 
 
-def multiply(s_ref, weights, blocks, shifts, o_ref, part, rows, acc, held, sem):
+def multiply(s_ref, weights, blocks, shifts, o_ref, part, rows, held, sem):
     x = s_ref[0]
     core = s_ref[1]
     chans, depth = weights[0].shape
@@ -114,21 +114,16 @@
         spot = lax.rem(x + shift, 4) * size + at
         rows[pl.ds(pl.multiple_of(spot, 32), ref.shape[0]), :] = ref[...]
     dims = (((1,), (1,)), ((), ()))
-    for k in range(depth // STEP):
-        at = slice(k * STEP, (k + 1) * STEP)
-        for half, ref in enumerate(weights):
-            spot = slice(half * chans, (half + 1) * chans)
-            value = mm(ref[:, at], rows[:, at], dims)
-            if k:
-                acc[spot, :] += value
-            else:
-                acc[spot, :] = value
+    lanes = pl.ds(part * rows.shape[0], rows.shape[0])
     copies = []
-    for half in range(2):
-        held[half] = acc[half * chans : (half + 1) * chans, :].astype(BF16)
+    for half, ref in enumerate(weights):
+        total = mm(ref[:, :STEP], rows[:, :STEP], dims)
+        for k in range(1, depth // STEP):
+            at = slice(k * STEP, (k + 1) * STEP)
+            total = total + mm(ref[:, at], rows[:, at], dims)
+        held[half] = total.astype(BF16)
         to = core if half == 0 else 1 - core
         at = pl.ds(pl.multiple_of(to * chans, chans), chans)
-        lanes = pl.ds(part * rows.shape[0], rows.shape[0])
         copies.append(
             pltpu.make_async_copy(held.at[half], o_ref.at[at, lanes], sem.at[half])
         )
@@ -140,18 +135,18 @@
 def first_body(s_ref, *refs, shifts):
     count = len(shifts)
     weights, blocks, later = refs[:2], refs[2 : 2 + count], refs[2 + count]
-    o_ref, keep_ref, rows, acc, held, sem = refs[3 + count :]
+    o_ref, keep_ref, rows, held, sem = refs[3 + count :]
     keep = pltpu.make_async_copy(later, keep_ref, sem.at[2])
     keep.start()
-    multiply(s_ref, weights, blocks, shifts, o_ref, 0, rows, acc, held, sem)
+    multiply(s_ref, weights, blocks, shifts, o_ref, 0, rows, held, sem)
     keep.wait()
 
 
 def second_body(s_ref, *refs, shifts):
     count = len(shifts)
     weights, blocks = refs[:2], refs[2 : 2 + count]
-    o_ref, rows, acc, held, sem = refs[3 + count :]
-    multiply(s_ref, weights, blocks, shifts, o_ref, 1, rows, acc, held, sem)
+    o_ref, rows, held, sem = refs[3 + count :]
+    multiply(s_ref, weights, blocks, shifts, o_ref, 1, rows, held, sem)
 
 
 def project(spots, own, other, blocks, shifts, later=None, g=None):
@@ -176,7 +171,6 @@
         input_output_aliases=aliases,
         scratch_shapes=[
             pltpu.VMEM((rows, depth), BF16),
-            pltpu.VMEM((2 * chans, rows), F32),
             pltpu.VMEM((2, chans, rows), BF16),
             pltpu.SemaphoreType.DMA((3,)),
         ],
@@ -306,7 +300,7 @@
             pltpu.VMEM((2 * nb + 1 - EARLY, TILE, TILE), BF16),
         ],
         name="convolve",
-        compiler_params=params(),
+        compiler_params=pltpu.CompilerParams(vmem_limit_bytes=VMEM_MIB * 2**20),
         cost_estimate=cost(6 * 10**9, 4 * 10**6),
     )(spot, g, xt, tiles, taps)
 

time: 88.3 us -> 88.3 us (level)
  no operation moved by 1% of the time
where the time goes in v5:
time: 88.3 us; the launch traced here: 87.8 us
  starting transfers between devices  28.5 us (32%)
  waiting for transfers between devices  22.4 us (25%)
  Pallas kernels  18.8 us (21%)
  blocking collectives  12.8 us (14%)
  local copies, waits for them, and re-layouts  4.44 us (5%)
    all_to_all x1, blocking collectives, on_device(): major = lax.all_to_all(major, seq, 0, 0, tiled=True)  12.8 us
    all_to_all x1, waiting for transfers between devices, on_device(): g = lax.all_to_all(g, ('core',) + seq, 0, 0, tiled=True)  8.69 us
    ppermute x1, waiting for transfers between devices, on_device(): before = lax.ppermute(grad_out, 'x', X_UP)  8.35 us
    pallas_call x2, Pallas kernels, project(): pl.pallas_call(functools.partial(body, shifts=shifts), out_shape=out, in_...  7.58 us
    pallas_call x1, Pallas kernels, convolve(): pl.pallas_call(conv_body, out_shape=jax.ShapeDtypeStruct((senders, 8 * wi...  6.53 us
    all_to_all x1, starting transfers between devices, on_device(): turned = lax.all_to_all(turned, seq, 0, 0, tiled=True)  5.94 us
    all_to_all x1, starting transfers between devices, on_device(): g = lax.all_to_all(g, ('core',) + seq, 0, 0, tiled=True)  4.37 us
    ppermute x1, starting transfers between devices, on_device(): near_own = lax.ppermute(grad_out, near, Z_NEAR)  4.15 us
  transfers between devices with their start and end apart: 12, of which 4 were waited for; matrix products, arithmetic and copies ran while one was open for 2% of the time, Pallas kernels for 13%

profile of v5, /device:TPU:0, one launch (start us, length us, event | category | flops | bytes accessed | tf_op | source)
XLA Modules:
  0.0 87.8 jit_solution(14396268318103746042)
XLA Ops:
  0.8 1.6 %collective-permute-start.1 = (bf16[64,4096]{1,0:T(8,128)(2,1)}, bf16[64,4096]{1,0:T(8,128)(2,1)S(1)}, u32[]{:S(2)}, u32[]{:S(2)}) collective-permute-start(bf16[64,4096]{1,0:T(8,128)(2,1)} %refs_2_), channel_id=1, source_target_pairs={{0,2},{2,4},{4,6},{6,0},{1,3},{3,5},{5,7},{7,1},{8,10},{10,12},{12... | collective-permute-start | bytes 1572872 | tf_op jit(solution)/shard_map/ppermute | solution.py:351
  2.4 1.6 %collective-permute-start.2 = (bf16[64,4096]{1,0:T(8,128)(2,1)}, bf16[64,4096]{1,0:T(8,128)(2,1)S(1)}, u32[]{:S(2)}, u32[]{:S(2)}) collective-permute-start(bf16[64,4096]{1,0:T(8,128)(2,1)} %refs_2_), channel_id=1, source_target_pairs={{0,6},{2,0},{4,2},{6,4},{1,7},{3,1},{5,3},{7,5},{8,14},{10,8},{12,... | collective-permute-start | bytes 1572872 | tf_op jit(solution)/shard_map/ppermute | solution.py:352
  4.1 4.1 %collective-permute-start.5 = (bf16[64,4096]{1,0:T(8,128)(2,1)}, bf16[64,4096]{1,0:T(8,128)(2,1)}, u32[]{:S(2)}, u32[]{:S(2)}) collective-permute-start(bf16[64,4096]{1,0:T(8,128)(2,1)} %refs_2_), channel_id=1, source_target_pairs={{0,24},{8,16},{16,8},{24,0},{1,25},{9,17},{17,9},{25,1},{2,26},{10... | collective-permute-start | bytes 1572872 | tf_op jit(solution)/shard_map/ppermute | solution.py:353
  8.2 8.3 %collective-permute-done.1.refs_3_ = bf16[64,4096]{1,0:T(8,128)(2,1)S(1)} collective-permute-done((bf16[64,4096]{1,0:T(8,128)(2,1)}, bf16[64,4096]{1,0:T(8,128)(2,1)S(1)}, u32[]{:S(2)}, u32[]{:S(2)}) %collective-permute-start.1) | collective-permute-done | bytes 524320 | tf_op jit(solution)/shard_map/ppermute | solution.py:351
  16.6 0.7 slice.8
  17.7 0.7 slice.9
  18.4 2.8 %collective-permute-start.4 = (bf16[32,4096]{1,0:T(8,128)(2,1)}, bf16[32,4096]{1,0:T(8,128)(2,1)}, u32[]{:S(2)}, u32[]{:S(2)}) collective-permute-start(bf16[32,4096]{1,0:T(8,128)(2,1)} %slice.9), channel_id=1, source_target_pairs={{0,6},{2,0},{4,2},{6,4},{1,7},{3,1},{5,3},{7,5},{8,14},{10,8},{12,... | collective-permute-start | bytes 786440 | tf_op jit(solution)/shard_map/ppermute | solution.py:356
  21.3 3.2 %collective-permute-start.7 = (bf16[64,4096]{1,0:T(8,128)(2,1)}, bf16[64,4096]{1,0:T(8,128)(2,1)}, u32[]{:S(2)}, u32[]{:S(2)}) collective-permute-start(bf16[64,4096]{1,0:T(8,128)(2,1)} %collective-permute-done.5.refs_7_), channel_id=1, source_target_pairs={{0,6},{2,0},{4,2},{6,4},{1,7},{3,1},{5,3},{7,5},{8,14},{10,8},{12,... | collective-permute-start | bytes 1572872 | tf_op jit(solution)/shard_map/ppermute | solution.py:360
  24.5 1.0 %copy-done.4 = bf16[1024,256]{1,0:T(8,128)(2,1)S(1)} copy-done((bf16[1024,256]{1,0:T(8,128)(2,1)S(1)}, bf16[1024,256]{1,0:T(8,128)(2,1)}, u32[]{:S(2)}) %copy-start.4) | copy-done | bytes 524312
  25.5 1.4 %prep_input.1 = bf16[8,256,128]{2,1,0:T(8,128)(2,1)S(1)} custom-call(bf16[1024,256]{1,0:T(8,128)(2,1)S(1)} %copy-done.4), custom_call_target="tpu_custom_call" | custom-call | flops 2000000000 | bytes 1048576 | tf_op jit(solution)/shard_map/prep_input/pallas_call | solution.py:61
  26.9 0.8 copy-done.2
  27.7 5.9 %all-to-all-start.1 = ((bf16[8,256,128]{2,1,0:T(8,128)(2,1)}), bf16[8,256,128]{2,1,0:T(8,128)(2,1)}, u32[]{:S(2)}, u32[]{:S(2)}) async-start(bf16[8,256,128]{2,1,0:T(8,128)(2,1)} %copy-done.2), calls=%async_computation.1 | async-start | bytes 1048576 | tf_op jit(solution)/shard_map/all_to_all | solution.py:358
  33.7 4.1 %collective-permute-start.8 = (bf16[32,4096]{1,0:T(8,128)(2,1)S(1)}, bf16[32,4096]{1,0:T(8,128)(2,1)S(1)}, u32[]{:S(2)}, u32[]{:S(2)}) collective-permute-start(bf16[32,4096]{1,0:T(8,128)(2,1)S(1)} %collective-permute-done.3.refs_5_), channel_id=1, source_target_pairs={{0,24},{8,16},{16,8},{24,0},{1,25},{9,17},{17,9},{25,1},{2,26},{10... | collective-permute-start | bytes 786440 | tf_op jit(solution)/shard_map/ppermute | solution.py:361
  37.9 1.0 %copy-done.3 = bf16[64,4096]{1,0:T(8,128)(2,1)S(1)} copy-done((bf16[64,4096]{1,0:T(8,128)(2,1)S(1)}, bf16[64,4096]{1,0:T(8,128)(2,1)}, u32[]{:S(2)}) %copy-start.3) | copy-done | bytes 524312
  39.0 3.7 %project.2 = (bf16[512,512]{1,0:T(8,128)(2,1)}, bf16[64,4096]{1,0:T(8,128)(2,1)S(1)}) custom-call(s32[3]{0:T(128)S(1)} %pad_add_fusion.s_ref, bf16[256,4096]{1,0:T(8,128)(2,1)S(1)} %copy-done.1, bf16[256,4096]{1,0:T(8,128)(2,1)} %collective-permute-done.refs_1_, bf16[64,4096]{1,0:T(8,128)(2,1)S(1)} %copy-done.3, ...), custom_call_target="tpu_custom_call" | custom-call | flops 1073741824 | bytes 6291456 | tf_op jit(solution)/shard_map/project/pallas_call | solution.py:164
  42.7 2.3 %collective-permute-done.8.refs_5_ = bf16[32,4096]{1,0:T(8,128)(2,1)S(1)} collective-permute-done((bf16[32,4096]{1,0:T(8,128)(2,1)S(1)}, bf16[32,4096]{1,0:T(8,128)(2,1)S(1)}, u32[]{:S(2)}, u32[]{:S(2)}) %collective-permute-start.8) | collective-permute-done | bytes 262176 | tf_op jit(solution)/shard_map/ppermute | solution.py:361
  45.0 3.0 %collective-permute-done.9.refs_6_ = bf16[32,4096]{1,0:T(8,128)(2,1)S(1)} collective-permute-done((bf16[32,4096]{1,0:T(8,128)(2,1)}, bf16[32,4096]{1,0:T(8,128)(2,1)S(1)}, u32[]{:S(2)}, u32[]{:S(2)}) %collective-permute-start.9) | collective-permute-done | bytes 262176 | tf_op jit(solution)/shard_map/ppermute | solution.py:362
  48.0 3.9 %project.3 = bf16[512,512]{1,0:T(8,128)(2,1)} custom-call(s32[3]{0:T(128)S(1)} %pad_add_fusion.s_ref, bf16[256,4096]{1,0:T(8,128)(2,1)S(1)} %copy-done.1, bf16[256,4096]{1,0:T(8,128)(2,1)} %collective-permute-done.refs_1_, bf16[64,4096]{1,0:T(8,128)(2,1)S(1)} %get-tuple-element.10.refs_2_, ...), custom_call_target="tpu_custom_call", output_to_operand_aliasing={{}: (8, {})} | custom-call | flops 1073741824 | bytes 6291456 | tf_op jit(solution)/shard_map/project/pallas_call | solution.py:164
  51.9 4.4 %all-to-all-start = ((bf16[16,32,512]{2,1,0:T(8,128)(2,1)}), bf16[16,32,512]{2,1,0:T(8,128)(2,1)S(1)}, u32[]{:S(2)}, u32[]{:S(2)}) async-start(bf16[16,32,512]{2,1,0:T(8,128)(2,1)} %bitcast.3), calls=%async_computation | async-start | bytes 1048576 | tf_op jit(solution)/shard_map/all_to_all | solution.py:376
  56.4 2.3 %ready.1 = (bf16[56,128,128]{2,1,0:T(8,128)(2,1)S(1)}, bf16[256,1024]{1,0:T(8,128)(2,1)S(1)}) custom-call(bf16[64,128]{1,0:T(8,128)(2,1)S(1)} %bitcast.5, bf16[8,256,128]{2,1,0:T(8,128)(2,1)} %all-to-all-done.1.x_ref), custom_call_target="tpu_custom_call" | custom-call | flops 2000000000 | bytes 1835008 | tf_op jit(solution)/shard_map/ready/pallas_call | solution.py:94
  58.7 8.7 %all-to-all-done.g_ref = bf16[16,32,512]{2,1,0:T(8,128)(2,1)S(1)} async-done(((bf16[16,32,512]{2,1,0:T(8,128)(2,1)}), bf16[16,32,512]{2,1,0:T(8,128)(2,1)S(1)}, u32[]{:S(2)}, u32[]{:S(2)}) %all-to-all-start) | async-done | bytes 524320 | tf_op jit(solution)/shard_map/all_to_all | solution.py:376
  67.4 6.5 %convolve.1 = bf16[8,280,128]{2,1,0:T(8,128)(2,1)S(1)} custom-call(s32[3]{0:T(128)S(1)} %pad_add_fusion.s_ref, bf16[16,32,512]{2,1,0:T(8,128)(2,1)S(1)} %all-to-all-done.g_ref, bf16[256,1024]{1,0:T(8,128)(2,1)S(1)} %get-tuple-element.12.x_ref, bf16[56,128,128]{2,1,0:T(8,128)(2,1)S(1)} %get-tuple-element.13.t_ref, bf16[64,128]{1,0:T(8,128)(2,1)S(1)} %bitcast.6), custom_call_target="tpu_custom_call" | custom-call | flops 6000000000 | bytes 4000000 | tf_op jit(solution)/shard_map/convolve/pallas_call | solution.py:291
  73.9 12.8 %all_to_all.15.m_ref = bf16[8,280,128]{2,1,0:T(8,128)(2,1)S(1)} all-to-all(bf16[8,280,128]{2,1,0:T(8,128)(2,1)S(1)} %convolve.1), channel_id=1, replica_groups=mesh['y'=4,'zlo'=2,'zhi'=2,'x'=4,'core'=2] {'y','zlo'}, dimensions={0} | all-to-all | bytes 1146880 | tf_op jit(solution)/shard_map/all_to_all | solution.py:378
  86.8 1.0 %finish.1 = (bf16[1024,256]{1,0:T(8,128)(2,1)}, f32[8,1024]{1,0:T(8,128)}) custom-call(bf16[8,280,128]{2,1,0:T(8,128)(2,1)S(1)} %all_to_all.15.m_ref), custom_call_target="tpu_custom_call" | custom-call | flops 1000000 | bytes 1146880 | tf_op jit(solution)/shard_map/finish/pallas_call | solution.py:328
  (21 shorter events, 0.8 us)
Async XLA Ops:
  0.6 55.6 %copy-start = (bf16[8,8192]{1,0:T(8,128)(2,1)S(1)}, bf16[8,8192]{1,0:T(8,128)(2,1)}, u32[]{:S(2)}) copy-start(bf16[8,8192]{1,0:T(8,128)(2,1)} %param.7) | copy-start | bytes 393220
  0.6 37.3 %collective-permute-start = (bf16[256,4096]{1,0:T(8,128)(2,1)}, bf16[256,4096]{1,0:T(8,128)(2,1)}, u32[]{:S(2)}, u32[]{:S(2)}) collective-permute-start(bf16[256,4096]{1,0:T(8,128)(2,1)} %refs_0_.3), channel_id=1, source_target_pairs={{0,1},{1,0},{2,3},{3,2},{4,5},{5,4},{6,7},{7,6},{8,9},{9,8},{10,11... | collective-permute-start | bytes 6291464 | tf_op jit(solution)/shard_map/ppermute | solution.py:354
  0.8 15.7 %collective-permute-start.1 = (bf16[64,4096]{1,0:T(8,128)(2,1)}, bf16[64,4096]{1,0:T(8,128)(2,1)S(1)}, u32[]{:S(2)}, u32[]{:S(2)}) collective-permute-start(bf16[64,4096]{1,0:T(8,128)(2,1)} %refs_2_), channel_id=1, source_target_pairs={{0,2},{2,4},{4,6},{6,0},{1,3},{3,5},{5,7},{7,1},{8,10},{10,12},{12... | collective-permute-start | bytes 1572872 | tf_op jit(solution)/shard_map/ppermute | solution.py:351
  2.4 15.2 %collective-permute-start.2 = (bf16[64,4096]{1,0:T(8,128)(2,1)}, bf16[64,4096]{1,0:T(8,128)(2,1)S(1)}, u32[]{:S(2)}, u32[]{:S(2)}) collective-permute-start(bf16[64,4096]{1,0:T(8,128)(2,1)} %refs_2_), channel_id=1, source_target_pairs={{0,6},{2,0},{4,2},{6,4},{1,7},{3,1},{5,3},{7,5},{8,14},{10,8},{12,... | collective-permute-start | bytes 1572872 | tf_op jit(solution)/shard_map/ppermute | solution.py:352
  4.1 17.2 %collective-permute-start.5 = (bf16[64,4096]{1,0:T(8,128)(2,1)}, bf16[64,4096]{1,0:T(8,128)(2,1)}, u32[]{:S(2)}, u32[]{:S(2)}) collective-permute-start(bf16[64,4096]{1,0:T(8,128)(2,1)} %refs_2_), channel_id=1, source_target_pairs={{0,24},{8,16},{16,8},{24,0},{1,25},{9,17},{17,9},{25,1},{2,26},{10... | collective-permute-start | bytes 1572872 | tf_op jit(solution)/shard_map/ppermute | solution.py:353
  17.3 16.4 %collective-permute-start.3 = (bf16[32,4096]{1,0:T(8,128)(2,1)}, bf16[32,4096]{1,0:T(8,128)(2,1)S(1)}, u32[]{:S(2)}, u32[]{:S(2)}) collective-permute-start(bf16[32,4096]{1,0:T(8,128)(2,1)} %slice.8), channel_id=1, source_target_pairs={{0,2},{2,4},{4,6},{6,0},{1,3},{3,5},{5,7},{7,1},{8,10},{10,12},{12... | collective-permute-start | bytes 786440 | tf_op jit(solution)/shard_map/ppermute | solution.py:355
  18.4 19.4 %collective-permute-start.4 = (bf16[32,4096]{1,0:T(8,128)(2,1)}, bf16[32,4096]{1,0:T(8,128)(2,1)}, u32[]{:S(2)}, u32[]{:S(2)}) collective-permute-start(bf16[32,4096]{1,0:T(8,128)(2,1)} %slice.9), channel_id=1, source_target_pairs={{0,6},{2,0},{4,2},{6,4},{1,7},{3,1},{5,3},{7,5},{8,14},{10,8},{12,... | collective-permute-start | bytes 786440 | tf_op jit(solution)/shard_map/ppermute | solution.py:356
  21.3 26.7 %collective-permute-start.6 = (bf16[64,4096]{1,0:T(8,128)(2,1)}, bf16[64,4096]{1,0:T(8,128)(2,1)}, u32[]{:S(2)}, u32[]{:S(2)}) collective-permute-start(bf16[64,4096]{1,0:T(8,128)(2,1)} %collective-permute-done.5.refs_7_), channel_id=1, source_target_pairs={{0,2},{2,4},{4,6},{6,0},{1,3},{3,5},{5,7},{7,1},{8,10},{10,12},{12... | collective-permute-start | bytes 1572872 | tf_op jit(solution)/shard_map/ppermute | solution.py:359
  21.3 26.7 %collective-permute-start.7 = (bf16[64,4096]{1,0:T(8,128)(2,1)}, bf16[64,4096]{1,0:T(8,128)(2,1)}, u32[]{:S(2)}, u32[]{:S(2)}) collective-permute-start(bf16[64,4096]{1,0:T(8,128)(2,1)} %collective-permute-done.5.refs_7_), channel_id=1, source_target_pairs={{0,6},{2,0},{4,2},{6,4},{1,7},{3,1},{5,3},{7,5},{8,14},{10,8},{12,... | collective-permute-start | bytes 1572872 | tf_op jit(solution)/shard_map/ppermute | solution.py:360
  24.5 1.0 %copy-start.4 = (bf16[1024,256]{1,0:T(8,128)(2,1)S(1)}, bf16[1024,256]{1,0:T(8,128)(2,1)}, u32[]{:S(2)}) copy-start(bf16[1024,256]{1,0:T(8,128)(2,1)} %x_ref.1) | copy-start | bytes 1572868
  25.5 12.4 %copy-start.1 = (bf16[256,4096]{1,0:T(8,128)(2,1)S(1)}, bf16[256,4096]{1,0:T(8,128)(2,1)}, u32[]{:S(2)}) copy-start(bf16[256,4096]{1,0:T(8,128)(2,1)} %refs_0_.3) | copy-start | bytes 6291460
  26.9 0.8 copy-start.2
  27.7 24.1 %all-to-all-start.1 = ((bf16[8,256,128]{2,1,0:T(8,128)(2,1)}), bf16[8,256,128]{2,1,0:T(8,128)(2,1)}, u32[]{:S(2)}, u32[]{:S(2)}) async-start(bf16[8,256,128]{2,1,0:T(8,128)(2,1)} %copy-done.2), calls=%async_computation.1 | async-start | bytes 1048576 | tf_op jit(solution)/shard_map/all_to_all | solution.py:358
  33.7 11.3 %collective-permute-start.8 = (bf16[32,4096]{1,0:T(8,128)(2,1)S(1)}, bf16[32,4096]{1,0:T(8,128)(2,1)S(1)}, u32[]{:S(2)}, u32[]{:S(2)}) collective-permute-start(bf16[32,4096]{1,0:T(8,128)(2,1)S(1)} %collective-permute-done.3.refs_5_), channel_id=1, source_target_pairs={{0,24},{8,16},{16,8},{24,0},{1,25},{9,17},{17,9},{25,1},{2,26},{10... | collective-permute-start | bytes 786440 | tf_op jit(solution)/shard_map/ppermute | solution.py:361
  37.8 10.1 %collective-permute-start.9 = (bf16[32,4096]{1,0:T(8,128)(2,1)}, bf16[32,4096]{1,0:T(8,128)(2,1)S(1)}, u32[]{:S(2)}, u32[]{:S(2)}) collective-permute-start(bf16[32,4096]{1,0:T(8,128)(2,1)} %collective-permute-done.4.refs_6_), channel_id=1, source_target_pairs={{0,24},{8,16},{16,8},{24,0},{1,25},{9,17},{17,9},{25,1},{2,26},{10... | collective-permute-start | bytes 786440 | tf_op jit(solution)/shard_map/ppermute | solution.py:362
  37.9 1.0 %copy-start.3 = (bf16[64,4096]{1,0:T(8,128)(2,1)S(1)}, bf16[64,4096]{1,0:T(8,128)(2,1)}, u32[]{:S(2)}) copy-start(bf16[64,4096]{1,0:T(8,128)(2,1)} %refs_2_) | copy-start | bytes 1572868
  51.9 15.5 %all-to-all-start = ((bf16[16,32,512]{2,1,0:T(8,128)(2,1)}), bf16[16,32,512]{2,1,0:T(8,128)(2,1)S(1)}, u32[]{:S(2)}, u32[]{:S(2)}) async-start(bf16[16,32,512]{2,1,0:T(8,128)(2,1)} %bitcast.3), calls=%async_computation | async-start | bytes 1048576 | tf_op jit(solution)/shard_map/all_to_all | solution.py:376
